TPU v7x, 256 devices: a whole 4x4x8 slice. The times are simulated.
256 devices in a mesh: pair: 2 (over z_lo), ctx: 16 (over x, y), head: 8 (over z_hi, core).
Axes of the slice: x: 4, y: 4, z: 8 (z_hi: 4, z_lo: 2; z = z_hi * 2 + z_lo), core: 2. Of those that a mesh axis runs over, the one named last changes fastest.
Arguments:
- prompt_queries: bfloat16 [2048, 8192], P(('pair', 'ctx'), 'head'), may hold values from -128 to 128
- prompt_key_rows: bfloat16 [2048, 1024], P(('pair', 'ctx'), 'head'), may hold values from -8 to 8
- prompt_value_rows: bfloat16 [2048, 1024], P(('pair', 'ctx'), 'head'), may hold values from -6 to 6
- answer_queries: bfloat16 [2, 1024, 8192], P('pair', 'ctx', 'head'), may hold values from -128 to 128
- response_key_rows: bfloat16 [2, 1024, 1024], P('pair', 'ctx', 'head'), may hold values from -8 to 8
- response_value_rows: bfloat16 [2, 1024, 1024], P('pair', 'ctx', 'head'), may hold values from -6 to 6
- prompt_cotangent: bfloat16 [2048, 8192], P(('pair', 'ctx'), 'head'), may hold values from -6 to 6
- answer_cotangent: bfloat16 [2, 1024, 8192], P('pair', 'ctx', 'head'), may hold values from -6 to 6
- prompt_length: int32 [1], replicated, may hold values from 1025 to 2048
- answer_lengths: int32 [2], replicated, may hold values from 513 to 1024
Outputs:
- prompt_attended: bfloat16 [2048, 8192], P(('pair', 'ctx'), 'head')
- answer_attended: bfloat16 [2, 1024, 8192], P('pair', 'ctx', 'head')
- prompt_query_grad: bfloat16 [2048, 8192], P(('pair', 'ctx'), 'head')
- prompt_key_gradient: bfloat16 [2048, 1024], P(('pair', 'ctx'), 'head')
- prompt_value_gradient: bfloat16 [2048, 1024], P(('pair', 'ctx'), 'head')
- answer_query_grad: bfloat16 [2, 1024, 8192], P('pair', 'ctx', 'head')
- response_key_gradient: bfloat16 [2, 1024, 1024], P('pair', 'ctx', 'head')
- response_value_gradient: bfloat16 [2, 1024, 1024], P('pair', 'ctx', 'head')
All inputs are finite; a program needn't handle non-finite values.
Results may differ from a plain program's by a relative error of at most 0.0054.
Values may be sent and summed in bfloat16 or wider, within the bound.
No kernel may reach another device: no remote copies, remote signals or barrier semaphores. Data moves between devices by JAX's collectives and lax.ppermute only.
A program may use at most 64 MiB of HBM per device.

v0:
```python
import jax
import jax.numpy as jnp
from jax import lax
from jax.sharding import PartitionSpec as P

QUERY_HEADS = 64
KEY_VALUE_HEADS = 8
HEAD_SIZE = 128


NEGATIVE = -1e30


def in_one_piece(arrays, axis, dim, along):
    widths = [a.shape[along] for a in arrays]
    both = jnp.concatenate(arrays, axis=along)
    whole = lax.all_gather(both, axis, axis=dim, tiled=True)
    return tuple(jnp.split(whole, [sum(widths[:k]) for k in range(1, len(widths))], axis=along))


def in_blocks(array, dim, count):
    before, after = (array.shape[:dim], array.shape[dim + 1 :])
    return jnp.moveaxis(array.reshape(*before, count, -1, *after), dim, 0)


def summed_on_arrival(array, axis, dim):
    pieces = in_blocks(array, dim, lax.axis_size(axis))
    arrived = lax.all_to_all(pieces, axis, split_axis=0, concat_axis=0, tiled=True)
    return arrived.sum(axis=0)


def sent_together(arrays, axis, dim, along):
    widths = [a.shape[along] for a in arrays]
    both = jnp.concatenate(arrays, axis=along)
    whole = summed_on_arrival(both, axis, dim)
    return tuple(jnp.split(whole, [sum(widths[:k]) for k in range(1, len(widths))], axis=along))


def sent_together_2(arrays, axis, dim, along):
    ends, at = ([], 0)
    for a in arrays[:-1]:
        at += a.shape[along]
        ends.append(at)
    both = jnp.concatenate(arrays, axis=along)
    return tuple(
        jnp.split(lax.psum_scatter(both, axis, scatter_dimension=dim, tiled=True), ends, axis=along)
    )


def block_scores(queries, key_block, allowed, scaling):
    scores = (
        jnp.einsum("qcgd,kcd->cgqk", queries, key_block, preferred_element_type=jnp.float32)
        * scaling
    )
    return jnp.where(allowed[None, None], scores, NEGATIVE)


def statistic_block(carried, scores, allowed):
    run_max, run_sum = carried
    new_max = jnp.maximum(run_max, jnp.max(scores, axis=3))
    terms = jnp.where(allowed[None, None], jnp.exp(scores - new_max[..., None]), 0.0)
    return (new_max, run_sum * jnp.exp(run_max - new_max) + jnp.sum(terms, axis=3))


def value_block_add(accum, scores, allowed, row_max, value_block):
    probs = jnp.where(allowed[None, None], jnp.exp(scores - row_max[..., None]), 0.0).astype(
        jnp.bfloat16
    )
    return accum + jnp.einsum(
        "cgqk,kcd->cgqd", probs, value_block, preferred_element_type=jnp.float32
    )


def shares_of(scores, allowed, log_total):
    return jnp.where(allowed[None, None], jnp.exp(scores - log_total[..., None]), 0.0)


def body(
    prompt_queries,
    prompt_key_rows,
    prompt_value_rows,
    answer_queries,
    response_key_rows,
    response_value_rows,
    prompt_cotangent,
    answer_cotangent,
    prompt_length,
    answer_lengths,
):
    query_group_count = QUERY_HEADS // KEY_VALUE_HEADS
    local_heads = prompt_key_rows.shape[1] // HEAD_SIZE
    prompt_rows = prompt_queries.shape[0]
    response_row_count = answer_queries.shape[1]
    all_rows = prompt_rows + response_row_count
    ctx_devices = lax.axis_size("ctx")
    prompt_total = prompt_rows * lax.axis_size("pair") * ctx_devices
    answer_total = response_row_count * ctx_devices
    prompt_block = min(256, prompt_total)
    answer_block = min(256, answer_total)
    scaling = HEAD_SIZE ** (-0.5)
    pair_index = lax.axis_index("pair")
    ctx_index = lax.axis_index("ctx")
    prompt_len = prompt_length[0]
    answer_len = lax.dynamic_index_in_dim(answer_lengths, pair_index, keepdims=False)
    prompt_first = (pair_index * ctx_devices + ctx_index) * prompt_rows
    answer_first = ctx_index * response_row_count
    prompt_pos = prompt_first + jnp.arange(prompt_rows, dtype=jnp.int32)
    answer_pos = answer_first + jnp.arange(response_row_count, dtype=jnp.int32)
    reach = jnp.concatenate([prompt_pos, jnp.full((response_row_count,), prompt_total, jnp.int32)])
    valid_rows = jnp.concatenate([prompt_pos < prompt_len, answer_pos < answer_len])
    queries = jnp.concatenate([prompt_queries, answer_queries[0]], axis=0).reshape(
        all_rows, local_heads, query_group_count, HEAD_SIZE
    )
    later_queries = queries[prompt_rows:]
    cotangent = jnp.concatenate([prompt_cotangent, answer_cotangent[0]], axis=0).reshape(
        all_rows, local_heads, query_group_count, HEAD_SIZE
    )
    cotangent = jnp.where(valid_rows[:, None, None, None], cotangent, jnp.zeros_like(cotangent))
    later_cotangent = cotangent[prompt_rows:]
    prompt_pairs = in_one_piece((prompt_key_rows, prompt_value_rows), ("pair", "ctx"), 0, 1)
    answer_pairs = in_one_piece((response_key_rows[0], response_value_rows[0]), "ctx", 0, 1)
    prompt_blocks = (prompt_len + prompt_block - 1) // prompt_block
    answer_blocks = (
        jnp.minimum(answer_len, answer_first + response_row_count) + answer_block - 1
    ) // answer_block

    def prompt_allowed(first_key):
        key_pos = first_key + jnp.arange(prompt_block, dtype=jnp.int32)
        return (key_pos[None, :] <= reach[:, None]) & (key_pos[None, :] < prompt_len)

    def answer_allowed(first_key):
        key_pos = first_key + jnp.arange(answer_block, dtype=jnp.int32)
        return (key_pos[None, :] <= answer_pos[:, None]) & (key_pos[None, :] < answer_len)

    def take_block(source, first_key, size):
        return lax.dynamic_slice_in_dim(source, first_key, size, 0).reshape(
            size, local_heads, HEAD_SIZE
        )

    def prompt_statistic(index, carried):
        first_key = index * prompt_block
        allowed = prompt_allowed(first_key)
        scores = block_scores(
            queries, take_block(prompt_pairs[0], first_key, prompt_block), allowed, scaling
        )
        return statistic_block(carried, scores, allowed)

    def answer_statistic(index, carried):
        first_key = index * answer_block
        allowed = answer_allowed(first_key)
        scores = block_scores(
            later_queries, take_block(answer_pairs[0], first_key, answer_block), allowed, scaling
        )
        return statistic_block(carried, scores, allowed)

    stat_shape = (local_heads, query_group_count, all_rows)
    run_max, run_sum = lax.fori_loop(
        0,
        prompt_blocks,
        prompt_statistic,
        (jnp.full(stat_shape, NEGATIVE, jnp.float32), jnp.zeros(stat_shape, jnp.float32)),
    )
    tail_max, tail_sum = lax.fori_loop(
        0,
        answer_blocks,
        answer_statistic,
        (run_max[:, :, prompt_rows:], run_sum[:, :, prompt_rows:]),
    )
    row_max = jnp.concatenate([run_max[:, :, :prompt_rows], tail_max], axis=2)
    row_total = jnp.concatenate([run_sum[:, :, :prompt_rows], tail_sum], axis=2)
    later_max = row_max[:, :, prompt_rows:]

    def prompt_values(index, accum):
        first_key = index * prompt_block
        allowed = prompt_allowed(first_key)
        scores = block_scores(
            queries, take_block(prompt_pairs[0], first_key, prompt_block), allowed, scaling
        )
        return value_block_add(
            accum, scores, allowed, row_max, take_block(prompt_pairs[1], first_key, prompt_block)
        )

    def answer_values(index, accum):
        first_key = index * answer_block
        allowed = answer_allowed(first_key)
        scores = block_scores(
            later_queries, take_block(answer_pairs[0], first_key, answer_block), allowed, scaling
        )
        return value_block_add(
            accum, scores, allowed, later_max, take_block(answer_pairs[1], first_key, answer_block)
        )

    accum = lax.fori_loop(
        0,
        prompt_blocks,
        prompt_values,
        jnp.zeros((local_heads, query_group_count, all_rows, HEAD_SIZE), jnp.float32),
    )
    tail_accum = lax.fori_loop(0, answer_blocks, answer_values, accum[:, :, prompt_rows:])
    accum = jnp.concatenate([accum[:, :, :prompt_rows], tail_accum], axis=2)
    log_total = row_max + jnp.log(row_total)
    later_total = log_total[:, :, prompt_rows:]
    output = accum / row_total[..., None]
    attended = (
        jnp.where(valid_rows[None, None, :, None], output, 0.0)
        .transpose(2, 0, 1, 3)
        .reshape(all_rows, local_heads * query_group_count * HEAD_SIZE)
        .astype(jnp.bfloat16)
    )
    row_delta = jnp.sum(cotangent.astype(jnp.float32).transpose(1, 2, 0, 3) * output, axis=3)
    later_delta = row_delta[:, :, prompt_rows:]

    def backward_block(
        carried,
        first_key,
        size,
        allowed,
        key_source,
        value_source,
        rows_queries,
        rows_cotangent,
        rows_total,
        rows_delta,
    ):
        query_grad, key_grad, value_grad = carried
        key_block = take_block(key_source, first_key, size)
        value_block = take_block(value_source, first_key, size)
        scores = block_scores(rows_queries, key_block, allowed, scaling)
        shares = shares_of(scores, allowed, rows_total)
        weights = shares.astype(jnp.bfloat16)
        prob_grad = jnp.einsum(
            "qcgd,kcd->cgqk", rows_cotangent, value_block, preferred_element_type=jnp.float32
        )
        score_grad = (shares * (prob_grad - rows_delta[..., None])).astype(jnp.bfloat16)
        query_grad = query_grad + jnp.einsum(
            "cgqk,kcd->qcgd", score_grad, key_block, preferred_element_type=jnp.float32
        )
        key_part = (
            jnp.einsum(
                "cgqk,qcgd->kcd", score_grad, rows_queries, preferred_element_type=jnp.float32
            )
            * scaling
        )
        value_part = jnp.einsum(
            "cgqk,qcgd->kcd", weights, rows_cotangent, preferred_element_type=jnp.float32
        )
        key_grad = lax.dynamic_update_slice_in_dim(key_grad, key_part, first_key, 0)
        value_grad = lax.dynamic_update_slice_in_dim(value_grad, value_part, first_key, 0)
        return (query_grad, key_grad, value_grad)

    def prompt_backward(index, carried):
        first_key = index * prompt_block
        return backward_block(
            carried,
            first_key,
            prompt_block,
            prompt_allowed(first_key),
            prompt_pairs[0],
            prompt_pairs[1],
            queries,
            cotangent,
            log_total,
            row_delta,
        )

    def answer_backward(index, carried):
        first_key = index * answer_block
        return backward_block(
            carried,
            first_key,
            answer_block,
            answer_allowed(first_key),
            answer_pairs[0],
            answer_pairs[1],
            later_queries,
            later_cotangent,
            later_total,
            later_delta,
        )

    grad_shape = (all_rows, local_heads, query_group_count, HEAD_SIZE)
    query_grad, prompt_kgrad, prompt_vgrad = lax.fori_loop(
        0,
        prompt_blocks,
        prompt_backward,
        (
            jnp.zeros(grad_shape, jnp.float32),
            jnp.zeros((prompt_total, local_heads, HEAD_SIZE), jnp.float32),
            jnp.zeros((prompt_total, local_heads, HEAD_SIZE), jnp.float32),
        ),
    )
    later_qgrad, answer_kgrad, answer_vgrad = lax.fori_loop(
        0,
        answer_blocks,
        answer_backward,
        (
            jnp.zeros((response_row_count, local_heads, query_group_count, HEAD_SIZE), jnp.float32),
            jnp.zeros((answer_total, local_heads, HEAD_SIZE), jnp.float32),
            jnp.zeros((answer_total, local_heads, HEAD_SIZE), jnp.float32),
        ),
    )
    query_grad = query_grad + jnp.concatenate(
        [
            jnp.zeros((prompt_rows, local_heads, query_group_count, HEAD_SIZE), jnp.float32),
            later_qgrad,
        ],
        axis=0,
    )
    query_grad = (
        (query_grad * scaling)
        .reshape(all_rows, local_heads * query_group_count * HEAD_SIZE)
        .astype(jnp.bfloat16)
    )
    prompt_kgrad = prompt_kgrad.reshape(prompt_total, local_heads * HEAD_SIZE)
    prompt_vgrad = prompt_vgrad.reshape(prompt_total, local_heads * HEAD_SIZE)
    key_mine, value_mine = sent_together((prompt_kgrad, prompt_vgrad), ("pair", "ctx"), 0, 1)
    answer_key_mine, answer_value_mine = sent_together_2(
        (
            answer_kgrad.reshape(answer_total, local_heads * HEAD_SIZE),
            answer_vgrad.reshape(answer_total, local_heads * HEAD_SIZE),
        ),
        "ctx",
        0,
        1,
    )
    return (
        attended[:prompt_rows],
        attended[prompt_rows:][None],
        query_grad[:prompt_rows],
        key_mine.astype(jnp.bfloat16),
        value_mine.astype(jnp.bfloat16),
        query_grad[prompt_rows:][None],
        answer_key_mine.astype(jnp.bfloat16)[None],
        answer_value_mine.astype(jnp.bfloat16)[None],
    )


def solution(mesh):
    placed = (
        P(("pair", "ctx"), "head"),
        P(("pair", "ctx"), "head"),
        P(("pair", "ctx"), "head"),
        P("pair", "ctx", "head"),
        P("pair", "ctx", "head"),
        P("pair", "ctx", "head"),
        P(("pair", "ctx"), "head"),
        P("pair", "ctx", "head"),
        P(),
        P(),
    )
    return jax.shard_map(
        body,
        mesh=mesh,
        in_specs=placed,
        out_specs=(
            P(("pair", "ctx"), "head"),
            P("pair", "ctx", "head"),
            P(("pair", "ctx"), "head"),
            P(("pair", "ctx"), "head"),
            P(("pair", "ctx"), "head"),
            P("pair", "ctx", "head"),
            P("pair", "ctx", "head"),
            P("pair", "ctx", "head"),
        ),
        check_vma=False,
    )
```

profile of v0, /device:TPU:160, one launch (start us, length us, event | category | flops | bytes accessed | tf_op | source)
XLA Modules:
  0.0 362.9 jit_solution(6101378660674406775)
XLA Ops:
  7.3 1.4 pad_maximum_fusion.3
  9.4 1.2 dynamic_slice.34
  11.3 0.9 copy.72
  12.2 0.9 copy.71
  14.7 25.1 %all_gather.7 = bf16[1024,256]{1,0:T(8,128)(2,1)S(1)} all-gather(bf16[64,256]{1,0:T(8,128)(2,1)S(1)} %pad_maximum_fusion.4), channel_id=1, replica_groups=mesh['pair'=2,'ctx'=16,'head'=8] {'ctx'}, dimensions={0}, use_global_device_ids=true | all-gather | bytes 557056 | tf_op jit(solution)/shard_map/all_gather | solution.py:17
  39.8 125.2 %all-gather.2.cloned.1.call-done = bf16[2048,256]{1,0:T(8,128)(2,1)} async-done(((bf16[64,256]{1,0:T(8,128)(2,1)}), bf16[2048,256]{1,0:T(8,128)(2,1)}) %all-gather.2.cloned.1.call-update) | async-done | bytes 1048592 | tf_op jit(solution)/shard_map/all_gather | solution.py:17
  165.0 1.3 fusion.133
  166.3 11.1 %while.75 = (s32[]{:T(128)}, f32[1,8,128]{2,1,0:T(8,128)S(1)}, f32[1,8,128]{2,1,0:T(8,128)S(1)}, s32[]{:T(128)}, s32[128]{0:T(128)S(1)}, /*index=5*/s32[]{:T(128...) while((s32[]{:T(128)}, f32[1,8,128]{2,1,0:T(8,128)S(1)}, ...), condition=%wide.region_3.4_spmd, body=%wide.region_0.3_spmd.sunk | while | flops 68750088 | bytes 2579635 | solution.py:157
  177.5 1.4 while.78
  179.1 12.3 %while.76 = (s32[]{:T(128)}, f32[1,8,128,128]{3,2,1,0:T(8,128)S(1)}, s32[]{:T(128)}, s32[128]{0:T(128)S(1)}, s32[]{:T(128)}, /*index=5*/bf16[2048,128]{1,0:T(8,1...) while((s32[]{:T(128)}, ...), condition=%wide.region_9.10_spmd, body=%wide.region_8.9_spmd.sunk | while | flops 135725824 | bytes 1515703 | solution.py:193
  192.3 1.2 while.79
  193.8 2.3 fusion.128
  196.7 39.6 %while.77 = (s32[]{:T(128)}, f32[128,1,8,128]{0,3,2,1:T(8,128)S(1)}, f32[2048,1,128]{2,0,1:T(8,128)S(1)}, f32[2048,1,128]{2,0,1:T(8,128)S(1)}, s32[]{:T(128)}, /...) while((s32[]{:T(128)}, ...), condition=%wide.region_14.15_spmd, body=%wide.region_13.14_spmd.sunk | while | flops 337871616 | bytes 7351531 | solution.py:282
  197.5 1.2 fusion.199
  198.8 1.1 fusion.200
  200.5 1.1 fusion.201
  202.5 1.2 fusion.199
  203.7 1.1 fusion.200
  205.4 1.1 fusion.201
  207.4 1.2 fusion.199
  208.6 1.1 fusion.200
  210.4 1.1 fusion.201
  212.3 1.2 fusion.199
  213.6 1.1 fusion.200
  215.3 1.1 fusion.201
  217.3 1.2 fusion.199
  218.5 1.1 fusion.200
  220.3 1.1 fusion.201
  222.2 1.2 fusion.199
  223.5 1.1 fusion.200
  225.2 1.1 fusion.201
  227.2 1.2 fusion.199
  228.4 1.1 fusion.200
  230.2 1.1 fusion.201
  232.1 1.2 fusion.199
  233.4 1.1 fusion.200
  235.1 1.1 fusion.201
  236.2 1.5 pad_maximum_fusion
  237.7 15.6 %all-to-all-start = ((f32[32,64,256]{2,1,0:T(8,128)}), f32[32,64,256]{2,1,0:T(8,128)S(1)}, u32[]{:S(2)}, u32[]{:S(2)}) async-start(f32[32,64,256]{2,1,0:T(8,128)} %pad_maximum_fusion), calls=%async_computation | async-start | bytes 4194304 | tf_op jit(solution)/shard_map/all_to_all | solution.py:28
  254.2 0.8 broadcast.394.clone
  255.1 4.3 %while.80 = (s32[]{:T(128)}, f32[64,1,8,128]{3,0,2,1:T(8,128)S(1)}, f32[1024,1,128]{2,0,1:T(8,128)}, f32[1024,1,128]{2,0,1:T(8,128)}, s32[]{:T(128)}, /*index=5*...) while((s32[]{:T(128)}, f32[64,1,8,128]{3,0,2,1:T(8,128)S(1)}, ...), condition=%wide.region_16.17_spmd.clone, body=%wide.region_15.16_spmd.clone.sunk | while | flops 168952640 | bytes 3908847 | solution.py:292
  256.2 1.1 fusion.220
  257.2 0.9 fusion.222
  258.2 0.9 fusion.223
  259.4 2.2 pad_maximum_fusion.1
  261.7 1.0 copy.61
  262.7 1.1 multiply_convert_fusion
  266.8 87.1 %reduce-scatter.2.cloned.1.call-done = f32[64,256]{1,0:T(8,128)} async-done(((f32[1024,256]{1,0:T(8,128)}), f32[64,256]{1,0:T(8,128)}) %reduce-scatter.2.cloned.1.call-update) | async-done | bytes 65552 | tf_op jit(solution)/shard_map/reduce_scatter | solution.py:46
  (228 shorter events, 46.5 us)
Async XLA Ops:
  7.2 6.1 %copy-start.6 = (bf16[64,1024]{1,0:T(8,128)(2,1)S(1)}, bf16[64,1024]{1,0:T(8,128)(2,1)}, u32[]{:S(2)}) copy-start(bf16[64,1024]{1,0:T(8,128)(2,1)} %param.28) | copy-start | bytes 393220
  7.2 6.1 %copy-start.7 = (bf16[1,64,1024]{2,1,0:T(8,128)(2,1)S(1)}, bf16[1,64,1024]{2,1,0:T(8,128)(2,1)}, u32[]{:S(2)}) copy-start(bf16[1,64,1024]{2,1,0:T(8,128)(2,1)} %param.29) | copy-start | bytes 393220
  7.2 7.5 %copy-start.9 = (bf16[1,64,128]{2,1,0:T(8,128)(2,1)S(1)}, bf16[1,64,128]{2,1,0:T(8,128)(2,1)}, u32[]{:S(2)}) copy-start(bf16[1,64,128]{2,1,0:T(8,128)(2,1)} %param.26) | copy-start | bytes 49156
  7.2 7.5 %copy-start.8 = (bf16[1,64,128]{2,1,0:T(8,128)(2,1)S(1)}, bf16[1,64,128]{2,1,0:T(8,128)(2,1)}, u32[]{:S(2)}) copy-start(bf16[1,64,128]{2,1,0:T(8,128)(2,1)} %param.27) | copy-start | bytes 49156
  7.2 157.8 %all-gather.2.cloned.1.call-start = ((), (), s32[]{:S(2)}) async-start(), calls=%async_computation.2 | async-start | bytes 1081344 | tf_op jit(solution)/shard_map/all_gather | solution.py:17
  191.3 0.8 copy-start.2
  191.3 1.0 copy-start.3
  191.7 2.1 copy-start.10
  193.5 2.7 copy-start
  193.5 2.9 copy-start.4
  237.7 17.3 %copy-start.1 = (bf16[1024,128]{1,0:T(8,128)(2,1)S(1)}, bf16[1024,128]{1,0:T(8,128)(2,1)}, u32[]{:S(2)}) copy-start(bf16[1024,128]{1,0:T(8,128)(2,1)} %copy-done) | copy-start | bytes 786436
  237.7 117.6 %all-to-all-start = ((f32[32,64,256]{2,1,0:T(8,128)}), f32[32,64,256]{2,1,0:T(8,128)S(1)}, u32[]{:S(2)}, u32[]{:S(2)}) async-start(f32[32,64,256]{2,1,0:T(8,128)} %pad_maximum_fusion), calls=%async_computation | async-start | bytes 4194304 | tf_op jit(solution)/shard_map/all_to_all | solution.py:28
  253.3 100.6 %reduce-scatter.2.cloned.1.call-start = ((), (), s32[]{:S(2)}) async-start(), calls=%async_computation.3 | async-start | bytes 1114112 | tf_op jit(solution)/shard_map/reduce_scatter | solution.py:46
  261.7 3.7 %copy-start.5 = (bf16[128,1,8,128]{3,2,0,1:T(8,128)(2,1)S(1)}, bf16[128,1,8,128]{3,2,0,1:T(8,128)(2,1)}, u32[]{:S(2)}) copy-start(bf16[128,1,8,128]{3,2,0,1:T(8,128)(2,1)} %get-tuple-element.666) | copy-start | bytes 786436
Sparse Core Ops, SparseCore 0:
  10.4 154.5 all-gather.1
  261.8 92.0 reduce-scatter.1
where the time goes:
time: 358 us; the launch traced here: 363 us
  waiting for transfers between devices  212 us (59%)
  matrix products  44.8 us (13%)
  other arithmetic  34.1 us (10%)
  blocking collectives  25.1 us (7%)
  between operations  15.8 us (4%)
  starting transfers between devices  15.7 us (4%)
  local copies, waits for them, and re-layouts  13.3 us (4%)
    all_gather x1, waiting for transfers between devices, in_one_piece(): whole = lax.all_gather(both, axis, axis=dim, tiled=True)  125 us
    reduce_scatter x1, waiting for transfers between devices, sent_together_2(): lax.psum_scatter(both, axis, scatter_dimension=dim, tiled=True)  87.1 us
    all_gather x1, blocking collectives, in_one_piece(): whole = lax.all_gather(both, axis, axis=dim, tiled=True)  25.1 us
    lt x24, other arithmetic, prompt_allowed(): key_pos[None, :] < prompt_len  15.7 us
    all_to_all x1, starting transfers between devices, summed_on_arrival(): lax.all_to_all(pieces, axis, split_axis=0, concat_axis=0, tiled=True)  15.6 us
    dot_general x18, matrix products, block_scores(): jnp.einsum('qcgd,kcd->cgqk', queries, key_block, preferred_element_type=j...  13.1 us
    dot_general x9, matrix products, backward_block(): jnp.einsum('qcgd,kcd->cgqk', rows_cotangent, value_block, preferred_eleme...  10.2 us
    dot_general x9, matrix products, backward_block(): jnp.einsum('cgqk,kcd->qcgd', score_grad, key_block, preferred_element_typ...  9.11 us
  transfers between devices with their start and end apart: 3, of which 2 were waited for; matrix products, arithmetic and copies ran while one was open for 5% of the time, Pallas kernels for 0%

commit v1 on v0

v1 whole, which is shorter than its diff:
```python
import jax
import jax.numpy as jnp
from jax import lax
from jax.experimental import pallas as pl
from jax.experimental.pallas import tpu as pltpu
from jax.sharding import PartitionSpec as P

QUERY_HEADS = 64
KEY_VALUE_HEADS = 8
GROUP = QUERY_HEADS // KEY_VALUE_HEADS
HEAD_SIZE = 128
NEGATIVE = -1e30
SCALING = HEAD_SIZE ** (-0.5)
LOG2E = 1.4426950408889634
TO_LOG2 = SCALING * LOG2E
CHUNK = 256
F32 = jnp.float32
BF16 = jnp.bfloat16
VMEM = pl.BlockSpec(memory_space=pltpu.VMEM)
SMEM = pl.BlockSpec(memory_space=pltpu.SMEM)
KEYS, VALUES = slice(0, HEAD_SIZE), slice(HEAD_SIZE, 2 * HEAD_SIZE)


def dot(a, b, ca, cb):
    return lax.dot_general(a, b, (((ca,), (cb,)), ((), ())), preferred_element_type=F32)


def at(chunk):
    return pl.ds(pl.multiple_of(chunk * CHUNK, CHUNK), CHUNK)


def chunks_of(count):
    return lax.div(count + (CHUNK - 1), CHUNK)


def head(h):
    return slice(h * HEAD_SIZE, (h + 1) * HEAD_SIZE)


class Place:
    def __init__(self, place, rows, half):
        pair, ctx, prompt_len, self.answer_len = (place[i] for i in range(4))
        self.first = ctx * rows
        self.prompt_first = pair * half + self.first
        self.prompt_len = prompt_len
        self.own_len = jnp.clip(prompt_len - pair * half, 1, half)
        self.other_len = jnp.clip(prompt_len - (1 - pair) * half, 1, half)
        self.own_chunks = chunks_of(self.own_len)
        self.other_chunks = chunks_of(self.other_len)
        self.answer_chunks = jnp.where(
            self.first < self.answer_len, chunks_of(self.first + rows), 0
        )
        lane = lax.broadcasted_iota(jnp.int32, (1, rows * GROUP), 1)
        causal = self.first + lax.rem(lane, rows)
        flat = jnp.zeros_like(causal)
        self.own_limit = jnp.concatenate([causal, flat + (self.own_len - 1)], axis=1)
        self.other_limit = jnp.concatenate(
            [flat + jnp.where(pair > 0, half, -1), flat + (self.other_len - 1)], axis=1
        )
        self.answer_limit = causal


def prepare_kernel(place, prompt_q, answer_q, prompt_do, answer_do, q_t, do_t, both_s, *, half):
    rows = prompt_q.shape[0]
    lanes = rows * GROUP
    where = Place(place, rows, half)
    for k, (q_ref, do_ref, first, length) in enumerate(
        (
            (prompt_q, prompt_do, where.prompt_first, where.prompt_len),
            (answer_q, answer_do, where.first, where.answer_len),
        )
    ):
        live = first + lax.broadcasted_iota(jnp.int32, (rows, HEAD_SIZE), 0) < length
        q_rows = jnp.concatenate([q_ref[:, head(h)] for h in range(GROUP)], axis=0)
        do_rows = jnp.concatenate(
            [
                jnp.where(live, do_ref[:, head(h)].astype(F32), 0.0).astype(BF16)
                for h in range(GROUP)
            ],
            axis=0,
        )
        side = slice(k * lanes, (k + 1) * lanes)
        both_s[side, KEYS] = q_rows
        both_s[side, VALUES] = do_rows
        q_t[:, side] = q_rows.T
        do_t[:, side] = do_rows.T


def block_of(kv, c, part, cols):
    rows = part.stop - part.start
    count = CHUNK // rows
    return kv[pl.ds(c * count, count), part, cols].reshape(CHUNK, HEAD_SIZE)


def put_block(dkv, c, part, dk, dv):
    rows = part.stop - part.start
    count = CHUNK // rows
    dkv[pl.ds(c * count, count), part, KEYS] = dk.astype(BF16).reshape(count, rows, HEAD_SIZE)
    dkv[pl.ds(c * count, count), part, VALUES] = dv.astype(BF16).reshape(count, rows, HEAD_SIZE)


def masked_scores(kv, c, part, q_t, limit):
    s = dot(block_of(kv, c, part, KEYS), q_t, 1, 0)
    key = lax.broadcasted_iota(jnp.int32, s.shape, 0)
    return jnp.where(key <= limit - c * CHUNK, s, NEGATIVE)


def score_pass(kv, part, q_t, side, limit, chunks, scores):
    def step(c, run):
        s = masked_scores(kv, c, part, q_t[:, side], limit)
        scores[at(c), :] = s
        for k in range(CHUNK // 8):
            run = jnp.maximum(run, s[k * 8 : (k + 1) * 8])
        return run

    start = jnp.full((8, side.stop - side.start), NEGATIVE, F32)
    return lax.fori_loop(0, chunks, step, start)


def value_pass(kv, part, side, row_max, chunks, scores, o_t):
    def step(c, sums):
        p = jnp.exp2(scores[at(c), :] * TO_LOG2 - row_max)
        for k in range(CHUNK // 8):
            sums = sums + p[k * 8 : (k + 1) * 8]
        scores[at(c), :] = p
        o_t[:, side] += dot(block_of(kv, c, part, VALUES), p.astype(BF16), 0, 0)
        return sums

    start = jnp.zeros((8, side.stop - side.start), F32)
    return jnp.sum(lax.fori_loop(0, chunks, step, start), axis=0, keepdims=True)


def gradients(kv, c, part, shares, side, do_t, both_s, delta, dkv, dq_t):
    dp = dot(block_of(kv, c, part, VALUES), do_t[:, side], 1, 0)
    ds = (shares * (dp - delta)).astype(BF16)
    put_block(
        dkv,
        c,
        part,
        dot(ds, both_s[side, KEYS], 1, 0) * SCALING,
        dot(shares.astype(BF16), both_s[side, VALUES], 1, 0),
    )
    dq_t[:, side] += dot(block_of(kv, c, part, KEYS), ds, 0, 0)


def blank(dkv, part, begin):
    def step(c, _):
        zero = jnp.zeros((CHUNK, HEAD_SIZE), F32)
        put_block(dkv, c, part, zero, zero)
        return 0

    lax.fori_loop(begin, dkv.shape[0] * (part.stop - part.start) // CHUNK, step, 0)


def write_rows(ref, block_t, rows, first=None, length=None):
    block = block_t.T
    for h in range(GROUP):
        piece = block[h * rows : (h + 1) * rows]
        if first is not None:
            live = first + lax.broadcasted_iota(jnp.int32, (rows, HEAD_SIZE), 0) < length
            piece = jnp.where(live, piece, 0.0)
        ref[:, head(h)] = piece.astype(BF16)


def sides(q_t):
    lanes = q_t.shape[1] // 2
    return slice(0, lanes), slice(lanes, 2 * lanes), slice(0, 2 * lanes)


def own_forward_kernel(place, q_t, kv, o_t, stats, shared, own):
    rows = kv.shape[1] // 2
    prompt, answer, every = sides(q_t)
    where = Place(place, rows, kv.shape[0] * rows)
    upper, lower = slice(0, rows), slice(rows, 2 * rows)
    run = score_pass(kv, upper, q_t, every, where.own_limit, where.own_chunks, shared)
    own_run = score_pass(kv, lower, q_t, answer, where.answer_limit, where.answer_chunks, own)
    run = jnp.concatenate([run[:, prompt], jnp.maximum(run[:, answer], own_run)], axis=1)
    row_max = jnp.max(run, axis=0, keepdims=True) * TO_LOG2
    o_t[...] = jnp.zeros_like(o_t)
    total = value_pass(kv, upper, every, row_max, where.own_chunks, shared, o_t)
    own_total = value_pass(
        kv, lower, answer, row_max[:, answer], where.answer_chunks, own, o_t
    )
    stats[0:1, :] = row_max
    stats[1:2, prompt] = total[:, prompt]
    stats[1:2, answer] = total[:, answer] + own_total


def other_kernel(
    place, q_t, do_t, both_s, kv, o_in, stats, prompt_out, answer_out, dkv, dq_t, factors, scores, o_t
):
    rows = kv.shape[1]
    prompt, answer, every = sides(q_t)
    where = Place(place, rows, kv.shape[0] * rows)
    part = slice(0, rows)
    chunks = where.other_chunks
    run = score_pass(kv, part, q_t, every, where.other_limit, chunks, scores)
    own_max = stats[0:1, :]
    row_max = jnp.maximum(jnp.max(run, axis=0, keepdims=True) * TO_LOG2, own_max)
    shrink = jnp.exp2(own_max - row_max)
    o_t[...] = o_in[...] * shrink
    total = value_pass(kv, part, every, row_max, chunks, scores, o_t) + stats[1:2, :] * shrink
    inverse = 1.0 / total
    out_t = o_t[...] * inverse
    delta = jnp.sum(do_t[...].astype(F32) * out_t, axis=0, keepdims=True)
    factors[0:1, :] = row_max + jnp.log(total) * LOG2E
    factors[1:2, :] = delta
    write_rows(prompt_out, out_t[:, prompt], rows, where.prompt_first, where.prompt_len)
    write_rows(answer_out, out_t[:, answer], rows, where.first, where.answer_len)
    dq_t[...] = jnp.zeros_like(dq_t)

    def step(c, _):
        shares = scores[at(c), :] * inverse
        gradients(kv, c, part, shares, every, do_t, both_s, delta, dkv, dq_t)
        return 0

    lax.fori_loop(0, chunks, step, 0)
    blank(dkv, part, chunks)


def own_backward_kernel(
    place, q_t, do_t, both_s, kv, factors, dq_in, prompt_dq, answer_dq, dkv, dq_t
):
    rows = kv.shape[1] // 2
    prompt, answer, every = sides(q_t)
    where = Place(place, rows, kv.shape[0] * rows)
    dq_t[...] = dq_in[...]

    def run(part, side, limit, chunks):
        log_total, delta = factors[0:1, side], factors[1:2, side]

        def step(c, _):
            s = masked_scores(kv, c, part, q_t[:, side], limit)
            shares = jnp.exp2(s * TO_LOG2 - log_total)
            gradients(kv, c, part, shares, side, do_t, both_s, delta, dkv, dq_t)
            return 0

        lax.fori_loop(0, chunks, step, 0)
        blank(dkv, part, chunks)

    run(slice(0, rows), every, where.own_limit, where.own_chunks)
    run(slice(rows, 2 * rows), answer, where.answer_limit, where.answer_chunks)
    write_rows(prompt_dq, dq_t[:, prompt] * SCALING, rows)
    write_rows(answer_dq, dq_t[:, answer] * SCALING, rows)


def call(kernel, name, arrays, outs, scratch, flops, mib):
    return pl.pallas_call(
        kernel,
        out_shape=[jax.ShapeDtypeStruct(*o) for o in outs],
        in_specs=[SMEM] + [VMEM] * (len(arrays) - 1),
        out_specs=[VMEM] * len(outs),
        scratch_shapes=[pltpu.VMEM(*s) for s in scratch],
        compiler_params=pltpu.CompilerParams(vmem_limit_bytes=mib * 1024 * 1024),
        cost_estimate=pl.CostEstimate(flops=flops, bytes_accessed=0, transcendentals=0),
        name=name,
    )(*arrays)


def copies_of(parts, count):
    rows = parts[0].shape[0]

    def kernel(pk, pv, ak, av, out, alone):
        alone[:, KEYS] = pk[...]
        alone[:, VALUES] = pv[...]
        for i in range(count):
            out[i, :rows, KEYS] = pk[...]
            out[i, :rows, VALUES] = pv[...]
            out[i, rows:, KEYS] = ak[...]
            out[i, rows:, VALUES] = av[...]

    return pl.pallas_call(
        kernel,
        out_shape=[
            jax.ShapeDtypeStruct((count, 2 * rows, 2 * HEAD_SIZE), BF16),
            jax.ShapeDtypeStruct((rows, 2 * HEAD_SIZE), BF16),
        ],
        in_specs=[VMEM] * 4,
        out_specs=[VMEM] * 2,
        compiler_params=pltpu.CompilerParams(vmem_limit_bytes=67043328),
        cost_estimate=pl.CostEstimate(flops=10**6, bytes_accessed=0, transcendentals=0),
        name="copies",
    )(*parts)


def exchanged(pieces):
    return lax.all_to_all(pieces, "ctx", split_axis=0, concat_axis=0, tiled=True)


def to_partner(block):
    count = lax.axis_size("pair")
    return lax.ppermute(block, "pair", [(i, count - 1 - i) for i in range(count)])


def body(
    prompt_queries,
    prompt_key_rows,
    prompt_value_rows,
    answer_queries,
    response_key_rows,
    response_value_rows,
    prompt_cotangent,
    answer_cotangent,
    prompt_length,
    answer_lengths,
):
    rows = prompt_queries.shape[0]
    lanes = rows * GROUP
    pair_index = lax.axis_index("pair")
    count = lax.axis_size("ctx")
    half = count * rows
    copies, alone = copies_of(
        (prompt_key_rows, prompt_value_rows, response_key_rows[0], response_value_rows[0]), count
    )
    own_kv = exchanged(copies)
    other = to_partner(alone)
    other_copies = jnp.broadcast_to(other[None], (count, *other.shape))
    place = jnp.stack(
        [
            pair_index,
            lax.axis_index("ctx"),
            prompt_length[0],
            lax.dynamic_index_in_dim(answer_lengths, pair_index, keepdims=False),
        ]
    ).astype(jnp.int32)
    wide, tall = (HEAD_SIZE, 2 * lanes), (2 * lanes, 2 * HEAD_SIZE)
    out = ((rows, GROUP * HEAD_SIZE), BF16)
    stat = ((8, 2 * lanes), F32)
    q_t, do_t, both_s = call(
        lambda *refs: prepare_kernel(*refs, half=half),
        "prepare",
        (place, prompt_queries, answer_queries[0], prompt_cotangent, answer_cotangent[0]),
        [(wide, BF16), (wide, BF16), (tall, BF16)],
        [],
        10**9,
        8,
    )
    own_kv, other_copies, q_t, do_t, both_s = lax.optimization_barrier(
        (own_kv, other_copies, q_t, do_t, both_s)
    )
    other_kv = exchanged(other_copies)
    flops = 2 * half * lanes * HEAD_SIZE
    o_t, stats = call(
        own_forward_kernel,
        "own_forward",
        (place, q_t, own_kv),
        [(wide, F32), stat],
        [((half, 2 * lanes), F32), ((half, lanes), F32)],
        8 * flops,
        16,
    )
    prompt_out, answer_out, other_dkv, dq_t, factors = call(
        other_kernel,
        "other",
        (place, q_t, do_t, both_s, other_kv, o_t, stats),
        [out, out, (other_kv.shape, BF16), (wide, F32), stat],
        [((half, 2 * lanes), F32), (wide, F32)],
        12 * flops,
        16,
    )
    other_sum = exchanged(other_dkv).astype(F32).sum(axis=0)
    prompt_dq, answer_dq, own_dkv = call(
        own_backward_kernel,
        "own_backward",
        (place, q_t, do_t, both_s, own_kv, factors, dq_t),
        [out, out, (own_kv.shape, BF16)],
        [(wide, F32)],
        18 * flops,
        16,
    )
    from_partner = to_partner(other_sum)
    own_sum = exchanged(own_dkv).astype(F32).sum(axis=0)
    prompt_grad = (own_sum[:rows] + from_partner).astype(BF16)
    answer_grad = own_sum[rows:].astype(BF16)
    return (
        prompt_out,
        answer_out[None],
        prompt_dq,
        prompt_grad[:, KEYS],
        prompt_grad[:, VALUES],
        answer_dq[None],
        answer_grad[None, :, KEYS],
        answer_grad[None, :, VALUES],
    )


def solution(mesh):
    prompt = P(("pair", "ctx"), "head")
    answer = P("pair", "ctx", "head")
    return jax.shard_map(
        body,
        mesh=mesh,
        in_specs=(prompt, prompt, prompt, answer, answer, answer, prompt, answer, P(), P()),
        out_specs=(prompt, answer, prompt, prompt, prompt, answer, answer, answer),
        check_vma=False,
    )
```

time: 358 us -> 83.2 us (0.23); the launches traced: 363 us -> 82 us
  waiting for transfers between devices: 212 us -> 42.2 us
  matrix products: 44.8 us -> 0 us
  other arithmetic: 34.1 us -> 0.96 us
  blocking collectives: 25.1 us -> 0 us
  Pallas kernels: 0 us -> 14.5 us
  between operations: 15.8 us -> 1.44 us
  local copies, waits for them, and re-layouts: 13.3 us -> 3.65 us
  starting transfers between devices: 15.7 us -> 19.3 us
    all_gather x1 -> x0, waiting for transfers between devices: 125 us -> none  [in_one_piece(): whole = lax.all_gather(both, axis, axis=dim, tiled=True)]
    reduce_scatter x1 -> x0, waiting for transfers between devices: 87.1 us -> none  [sent_together_2(): lax.psum_scatter(both, axis, scatter_dimension=dim, tiled=True)]
    dot_general x63 -> x0, matrix products: 44.8 us -> none  [the longest x18 13.1 us: block_scores(): jnp.einsum('qcgd,kcd->cgqk', queries, key_block, preferred_element_type=j...]
    all_to_all x1 -> x4, waiting for transfers between devices: 0.01 us -> 42 us  [exchanged(): lax.all_to_all(pieces, 'ctx', split_axis=0, concat_axis=0, tiled=True)]
    all_gather x1 -> x0, blocking collectives: 25.1 us -> none  [in_one_piece(): whole = lax.all_gather(both, axis, axis=dim, tiled=True)]
    lt x28 -> x0, other arithmetic: 18.3 us -> none  [the longest x24 15.7 us: prompt_allowed(): key_pos[None, :] < prompt_len]
    pallas_call x0 -> x5, Pallas kernels: none -> 14.5 us  [the longest x4 12.6 us: call(): pl.pallas_call(kernel, out_shape=[jax.ShapeDtypeStruct(*o) for o in outs]...]
    concatenate x6 -> x0, other arithmetic: 5.77 us -> none  [the longest x1 2.24 us: sent_together_2(): both = jnp.concatenate(arrays, axis=along)]
  transfers between devices with their start and end apart: 3 -> 6, of which waited for: 2 -> 5; matrix products, arithmetic and copies ran while one was open for 5% -> 3% of each run, Pallas kernels for 0% -> 7%
where the time goes in v1:
time: 83.2 us; the launch traced here: 82 us
  waiting for transfers between devices  42.2 us (51%)
  starting transfers between devices  19.3 us (23%)
  Pallas kernels  14.5 us (17%)
  local copies, waits for them, and re-layouts  3.65 us (4%)
  between operations  1.44 us (2%)
  other arithmetic  0.96 us (1%)
    all_to_all x4, waiting for transfers between devices, exchanged(): lax.all_to_all(pieces, 'ctx', split_axis=0, concat_axis=0, tiled=True)  42 us
    all_to_all x4, starting transfers between devices, exchanged(): lax.all_to_all(pieces, 'ctx', split_axis=0, concat_axis=0, tiled=True)  18.1 us
    pallas_call x4, Pallas kernels, call(): pl.pallas_call(kernel, out_shape=[jax.ShapeDtypeStruct(*o) for o in outs]...  12.6 us
    pallas_call x1, Pallas kernels, copies_of(): pl.pallas_call(kernel, out_shape=[jax.ShapeDtypeStruct((count, 2 * rows,...  1.91 us
  transfers between devices with their start and end apart: 6, of which 5 were waited for; matrix products, arithmetic and copies ran while one was open for 3% of the time, Pallas kernels for 7%

profile of v1, /device:TPU:160, one launch (start us, length us, event | category | flops | bytes accessed | tf_op | source)
XLA Modules:
  0.0 82.0 jit_solution(2597802954368311648)
XLA Ops:
  0.6 1.9 %copies.1 = (bf16[16,128,256]{2,1,0:T(8,128)(2,1)}, bf16[64,256]{1,0:T(8,128)(2,1)}) custom-call(bf16[64,128]{1,0:T(8,128)(2,1)} %pk.1, bf16[64,128]{1,0:T(8,128)(2,1)} %pv.1, bf16[64,128]{1,0:T(8,128)(2,1)} %bitcast.14, bf16[64,128]{1,0:T(8,128)(2,1)} %bitcast.15), custom_call_target="tpu_custom_call" | custom-call | flops 1000000 | tf_op jit(solution)/shard_map/copies/pallas_call | solution.py:272
  2.5 0.0 copy-start.7
  2.5 0.0 copy-start.8
  2.5 0.0 copy-start
  2.6 0.0 copy-start.1
  2.6 0.0 copy-start.2
  2.6 0.0 copy-start.3
  2.6 7.2 %all-to-all-start = ((bf16[16,128,256]{2,1,0:T(8,128)(2,1)}), bf16[16,128,256]{2,1,0:T(8,128)(2,1)S(1)}, u32[]{:S(2)}, u32[]{:S(2)}) async-start(bf16[16,128,256]{2,1,0:T(8,128)(2,1)} %get-tuple-element.28), calls=%async_computation | async-start | bytes 2097152 | tf_op jit(solution)/shard_map/all_to_all | solution.py:287
  9.8 0.0 copy-done.7
  9.8 1.1 %collective-permute-start = (bf16[64,256]{1,0:T(8,128)(2,1)S(1)}, bf16[64,256]{1,0:T(8,128)(2,1)S(1)}, u32[]{:S(2)}, u32[]{:S(2)}) collective-permute-start(bf16[64,256]{1,0:T(8,128)(2,1)S(1)} %copy-done.7), channel_id=1, source_target_pairs={{0,128},{128,0},{1,129},{129,1},{2,130},{130,2},{3,131},{131,3},{4... | collective-permute-start | bytes 98312 | tf_op jit(solution)/shard_map/ppermute | solution.py:292
  11.5 0.0 copy-done.8
  11.5 0.6 dynamic_slice.4
  12.1 0.7 pad_add_fusion.refs_0_.place
  12.9 0.0 copy-done
  12.9 0.0 copy-done.1
  12.9 0.0 copy-done.2
  12.9 0.0 copy-done.3
  12.9 0.8 prepare.1
  13.6 0.0 copy-start.4
  13.7 0.1 collective-permute-done
  13.8 13.7 %all-to-all-done.kv = bf16[16,128,256]{2,1,0:T(8,128)(2,1)S(1)} async-done(((bf16[16,128,256]{2,1,0:T(8,128)(2,1)}), bf16[16,128,256]{2,1,0:T(8,128)(2,1)S(1)}, u32[]{:S(2)}, u32[]{:S(2)}) %all-to-all-start) | async-done | bytes 1048608 | tf_op jit(solution)/shard_map/all_to_all | solution.py:287
  27.5 0.8 %broadcast_in_dim.18 = bf16[16,64,256]{2,1,0:T(8,128)(2,1)} broadcast(bf16[64,256]{1,0:T(8,128)(2,1)S(1)} %collective-permute-done), dimensions={1,2} | broadcast | bytes 557056 | tf_op jit(solution)/shard_map/broadcast_in_dim | solution.py:317
  28.4 0.0 copy-done.4
  28.4 3.6 %all-to-all-start.1 = ((bf16[16,64,256]{2,1,0:T(8,128)(2,1)}), bf16[16,64,256]{2,1,0:T(8,128)(2,1)S(1)}, u32[]{:S(2)}, u32[]{:S(2)}) async-start(bf16[16,64,256]{2,1,0:T(8,128)(2,1)} %broadcast_in_dim.18), calls=%async_computation.1 | async-start | bytes 1048576 | tf_op jit(solution)/shard_map/all_to_all | solution.py:287
  32.0 1.7 %own_forward.1 = (f32[128,1024]{1,0:T(8,128)S(1)}, f32[8,1024]{1,0:T(8,128)S(1)}) custom-call(s32[4]{0:T(128)S(1)} %pad_add_fusion.refs_0_.place, bf16[128,1024]{1,0:T(8,128)(2,1)S(1)} %get-tuple-element.33.q_t, bf16[16,128,256]{2,1,0:T(8,128)(2,1)S(1)} %all-to-all-done.kv), custom_call_target="tpu_custom_call" | custom-call | flops 1073741824 | tf_op jit(solution)/shard_map/own_forward/pallas_call | solution.py:248
  33.7 8.3 %all-to-all-done.1.kv = bf16[16,64,256]{2,1,0:T(8,128)(2,1)S(1)} async-done(((bf16[16,64,256]{2,1,0:T(8,128)(2,1)}), bf16[16,64,256]{2,1,0:T(8,128)(2,1)S(1)}, u32[]{:S(2)}, u32[]{:S(2)}) %all-to-all-start.1) | async-done | bytes 524320 | tf_op jit(solution)/shard_map/all_to_all | solution.py:287
  42.0 0.0 copy-start.5
  42.0 0.9 %copy-done.5 = bf16[128,1024]{1,0:T(8,128)(2,1)S(1)} copy-done((bf16[128,1024]{1,0:T(8,128)(2,1)S(1)}, bf16[128,1024]{1,0:T(8,128)(2,1)}, u32[]{:S(2)}) %copy-start.5) | copy-done | bytes 262168
  43.0 6.8 %other.1 = (bf16[64,1024]{1,0:T(8,128)(2,1)}, bf16[64,1024]{1,0:T(8,128)(2,1)}, bf16[16,64,256]{2,1,0:T(8,128)(2,1)}, f32[128,1024]{1,0:T(8,128)S(1)}, f32[8,1024]{1,0:T(8,128)S(1)}) custom-call(s32[4]{0:T(128)S(1)} %pad_add_fusion.refs_0_.place, bf16[128,1024]{1,0:T(8,128)(2,1)S(1)} %get-tuple-element.33.q_t, bf16[128,1024]{1,0:T(8,128)(2,1)S(1)} %copy-done.5, ...), custom_call_target="tpu_custom_call" | custom-call | flops 1610612736 | tf_op jit(solution)/shard_map/other/pallas_call | solution.py:248
  49.8 0.0 copy-start.6
  49.8 3.7 %all-to-all-start.3 = ((bf16[16,64,256]{2,1,0:T(8,128)(2,1)}), bf16[16,64,256]{2,1,0:T(8,128)(2,1)S(1)}, u32[]{:S(2)}, u32[]{:S(2)}) async-start(bf16[16,64,256]{2,1,0:T(8,128)(2,1)} %get-tuple-element.46), calls=%async_computation.3 | async-start | bytes 1048576 | tf_op jit(solution)/shard_map/all_to_all | solution.py:287
  53.5 0.0 copy-done.6
  53.5 3.3 %own_backward.1 = (bf16[64,1024]{1,0:T(8,128)(2,1)}, bf16[64,1024]{1,0:T(8,128)(2,1)}, bf16[16,128,256]{2,1,0:T(8,128)(2,1)}) custom-call(s32[4]{0:T(128)S(1)} %pad_add_fusion.refs_0_.place, bf16[128,1024]{1,0:T(8,128)(2,1)S(1)} %get-tuple-element.33.q_t, bf16[128,1024]{1,0:T(8,128)(2,1)S(1)} %copy-done.6, bf16[1024,256]{1,0:T(8,128)(2,1)S(1)} %get-tuple-element.35.both_s, ...), custom_call_target="tpu_custom_call" | custom-call | flops 2415919104 | tf_op jit(solution)/shard_map/own_backward/pallas_call | solution.py:248
  56.8 6.7 %all-to-all-done.3 = bf16[16,64,256]{2,1,0:T(8,128)(2,1)S(1)} async-done(((bf16[16,64,256]{2,1,0:T(8,128)(2,1)}), bf16[16,64,256]{2,1,0:T(8,128)(2,1)S(1)}, u32[]{:S(2)}, u32[]{:S(2)}) %all-to-all-start.3) | async-done | bytes 524320 | tf_op jit(solution)/shard_map/all_to_all | solution.py:287
  63.5 3.7 %all-to-all-start.2 = ((bf16[16,128,256]{2,1,0:T(8,128)(2,1)}), bf16[16,128,256]{2,1,0:T(8,128)(2,1)S(1)}, u32[]{:S(2)}, u32[]{:S(2)}) async-start(bf16[16,128,256]{2,1,0:T(8,128)(2,1)} %get-tuple-element.45), calls=%async_computation.2 | async-start | bytes 2097152 | tf_op jit(solution)/shard_map/all_to_all | solution.py:287
  67.2 0.1 convert_reduce_fusion.1
  67.3 0.1 collective-permute-start.1
  67.4 13.2 %all-to-all-done.2 = bf16[16,128,256]{2,1,0:T(8,128)(2,1)S(1)} async-done(((bf16[16,128,256]{2,1,0:T(8,128)(2,1)}), bf16[16,128,256]{2,1,0:T(8,128)(2,1)S(1)}, u32[]{:S(2)}, u32[]{:S(2)}) %all-to-all-start.2) | async-done | bytes 1048608 | tf_op jit(solution)/shard_map/all_to_all | solution.py:287
  80.6 0.1 convert_reduce_fusion
  80.7 0.6 slice_bitcast_fusion
  81.4 0.0 collective-permute-done.1
  81.4 0.6 fusion.1
  (2 shorter events, 0.0 us)
Async XLA Ops:
  2.5 7.2 %copy-start.7 = (bf16[64,256]{1,0:T(8,128)(2,1)S(1)}, bf16[64,256]{1,0:T(8,128)(2,1)}, u32[]{:S(2)}) copy-start(bf16[64,256]{1,0:T(8,128)(2,1)} %get-tuple-element.29) | copy-start | bytes 98308
  2.5 9.0 %copy-start.8 = (s32[2]{0:T(128)S(1)}, s32[2]{0:T(128)}, u32[]{:S(2)}) copy-start(s32[2]{0:T(128)} %param.19) | copy-start | bytes 28
  2.5 10.3 %copy-start = (bf16[64,1024]{1,0:T(8,128)(2,1)S(1)}, bf16[64,1024]{1,0:T(8,128)(2,1)}, u32[]{:S(2)}) copy-start(bf16[64,1024]{1,0:T(8,128)(2,1)} %refs_1_.1) | copy-start | bytes 393220
  2.6 10.3 %copy-start.1 = (bf16[1,64,1024]{2,1,0:T(8,128)(2,1)S(1)}, bf16[1,64,1024]{2,1,0:T(8,128)(2,1)}, u32[]{:S(2)}) copy-start(bf16[1,64,1024]{2,1,0:T(8,128)(2,1)} %param.13) | copy-start | bytes 393220
  2.6 10.3 %copy-start.2 = (bf16[64,1024]{1,0:T(8,128)(2,1)S(1)}, bf16[64,1024]{1,0:T(8,128)(2,1)}, u32[]{:S(2)}) copy-start(bf16[64,1024]{1,0:T(8,128)(2,1)} %refs_3_.1) | copy-start | bytes 393220
  2.6 10.3 %copy-start.3 = (bf16[1,64,1024]{2,1,0:T(8,128)(2,1)S(1)}, bf16[1,64,1024]{2,1,0:T(8,128)(2,1)}, u32[]{:S(2)}) copy-start(bf16[1,64,1024]{2,1,0:T(8,128)(2,1)} %param.17) | copy-start | bytes 393220
  2.6 24.9 %all-to-all-start = ((bf16[16,128,256]{2,1,0:T(8,128)(2,1)}), bf16[16,128,256]{2,1,0:T(8,128)(2,1)S(1)}, u32[]{:S(2)}, u32[]{:S(2)}) async-start(bf16[16,128,256]{2,1,0:T(8,128)(2,1)} %get-tuple-element.28), calls=%async_computation | async-start | bytes 2097152 | tf_op jit(solution)/shard_map/all_to_all | solution.py:287
  9.8 4.0 %collective-permute-start = (bf16[64,256]{1,0:T(8,128)(2,1)S(1)}, bf16[64,256]{1,0:T(8,128)(2,1)S(1)}, u32[]{:S(2)}, u32[]{:S(2)}) collective-permute-start(bf16[64,256]{1,0:T(8,128)(2,1)S(1)} %copy-done.7), channel_id=1, source_target_pairs={{0,128},{128,0},{1,129},{129,1},{2,130},{130,2},{3,131},{131,3},{4... | collective-permute-start | bytes 98312 | tf_op jit(solution)/shard_map/ppermute | solution.py:292
  13.6 14.7 %copy-start.4 = (bf16[128,1024]{1,0:T(8,128)(2,1)}, bf16[128,1024]{1,0:T(8,128)(2,1)S(1)}, u32[]{:S(2)}) copy-start(bf16[128,1024]{1,0:T(8,128)(2,1)S(1)} %get-tuple-element.34.do_t) | copy-start | bytes 786436
  28.4 13.6 %all-to-all-start.1 = ((bf16[16,64,256]{2,1,0:T(8,128)(2,1)}), bf16[16,64,256]{2,1,0:T(8,128)(2,1)S(1)}, u32[]{:S(2)}, u32[]{:S(2)}) async-start(bf16[16,64,256]{2,1,0:T(8,128)(2,1)} %broadcast_in_dim.18), calls=%async_computation.1 | async-start | bytes 1048576 | tf_op jit(solution)/shard_map/all_to_all | solution.py:287
  42.0 1.0 %copy-start.5 = (bf16[128,1024]{1,0:T(8,128)(2,1)S(1)}, bf16[128,1024]{1,0:T(8,128)(2,1)}, u32[]{:S(2)}) copy-start(bf16[128,1024]{1,0:T(8,128)(2,1)} %copy-done.4) | copy-start | bytes 786436
  49.8 3.7 %copy-start.6 = (bf16[128,1024]{1,0:T(8,128)(2,1)S(1)}, bf16[128,1024]{1,0:T(8,128)(2,1)}, u32[]{:S(2)}) copy-start(bf16[128,1024]{1,0:T(8,128)(2,1)} %copy-done.4) | copy-start | bytes 786436
  49.8 13.8 %all-to-all-start.3 = ((bf16[16,64,256]{2,1,0:T(8,128)(2,1)}), bf16[16,64,256]{2,1,0:T(8,128)(2,1)S(1)}, u32[]{:S(2)}, u32[]{:S(2)}) async-start(bf16[16,64,256]{2,1,0:T(8,128)(2,1)} %get-tuple-element.46), calls=%async_computation.3 | async-start | bytes 1048576 | tf_op jit(solution)/shard_map/all_to_all | solution.py:287
  63.5 17.0 %all-to-all-start.2 = ((bf16[16,128,256]{2,1,0:T(8,128)(2,1)}), bf16[16,128,256]{2,1,0:T(8,128)(2,1)S(1)}, u32[]{:S(2)}, u32[]{:S(2)}) async-start(bf16[16,128,256]{2,1,0:T(8,128)(2,1)} %get-tuple-element.45), calls=%async_computation.2 | async-start | bytes 2097152 | tf_op jit(solution)/shard_map/all_to_all | solution.py:287
  67.3 14.1 %collective-permute-start.1 = (f32[64,256]{1,0:T(8,128)S(1)}, f32[64,256]{1,0:T(8,128)S(1)}, u32[]{:S(2)}, u32[]{:S(2)}) collective-permute-start(f32[64,256]{1,0:T(8,128)S(1)} %convert_reduce_fusion.1), channel_id=1, source_target_pairs={{0,128},{128,0},{1,129},{129,1},{2,130},{130,2},{3,131},{131,3},{4... | collective-permute-start | bytes 196616 | tf_op jit(solution)/shard_map/ppermute | solution.py:292

commit v2 on v1

--- a/solution.py
+++ b/solution.py
@@ -60,8 +60,25 @@
         self.answer_limit = causal
 
 
-def prepare_kernel(place, prompt_q, answer_q, prompt_do, answer_do, q_t, do_t, both_s, *, half):
+def prepare_kernel(
+    place,
+    prompt_q,
+    answer_q,
+    prompt_do,
+    answer_do,
+    answer_k,
+    answer_v,
+    q_t,
+    do_t,
+    both_s,
+    answer_copies,
+    *,
+    half,
+):
     rows = prompt_q.shape[0]
+    for i in range(answer_copies.shape[0]):
+        answer_copies[i, :, KEYS] = answer_k[...]
+        answer_copies[i, :, VALUES] = answer_v[...]
     lanes = rows * GROUP
     where = Place(place, rows, half)
     for k, (q_ref, do_ref, first, length) in enumerate(
@@ -130,13 +147,13 @@
     return jnp.sum(lax.fori_loop(0, chunks, step, start), axis=0, keepdims=True)
 
 
-def gradients(kv, c, part, shares, side, do_t, both_s, delta, dkv, dq_t):
+def gradients(kv, c, part, shares, side, do_t, both_s, delta, dkv, out_part, dq_t):
     dp = dot(block_of(kv, c, part, VALUES), do_t[:, side], 1, 0)
     ds = (shares * (dp - delta)).astype(BF16)
     put_block(
         dkv,
         c,
-        part,
+        out_part,
         dot(ds, both_s[side, KEYS], 1, 0) * SCALING,
         dot(shares.astype(BF16), both_s[side, VALUES], 1, 0),
     )
@@ -167,27 +184,35 @@
     return slice(0, lanes), slice(lanes, 2 * lanes), slice(0, 2 * lanes)
 
 
-def own_forward_kernel(place, q_t, kv, o_t, stats, shared, own):
-    rows = kv.shape[1] // 2
-    prompt, answer, every = sides(q_t)
+def own_forward_kernel(place, q_t, kv, o_t, stats, scores):
+    rows = kv.shape[1]
+    every = sides(q_t)[2]
     where = Place(place, rows, kv.shape[0] * rows)
-    upper, lower = slice(0, rows), slice(rows, 2 * rows)
-    run = score_pass(kv, upper, q_t, every, where.own_limit, where.own_chunks, shared)
-    own_run = score_pass(kv, lower, q_t, answer, where.answer_limit, where.answer_chunks, own)
-    run = jnp.concatenate([run[:, prompt], jnp.maximum(run[:, answer], own_run)], axis=1)
+    part = slice(0, rows)
+    run = score_pass(kv, part, q_t, every, where.own_limit, where.own_chunks, scores)
     row_max = jnp.max(run, axis=0, keepdims=True) * TO_LOG2
     o_t[...] = jnp.zeros_like(o_t)
-    total = value_pass(kv, upper, every, row_max, where.own_chunks, shared, o_t)
-    own_total = value_pass(
-        kv, lower, answer, row_max[:, answer], where.answer_chunks, own, o_t
-    )
     stats[0:1, :] = row_max
-    stats[1:2, prompt] = total[:, prompt]
-    stats[1:2, answer] = total[:, answer] + own_total
+    stats[1:2, :] = value_pass(kv, part, every, row_max, where.own_chunks, scores, o_t)
 
 
 def other_kernel(
-    place, q_t, do_t, both_s, kv, o_in, stats, prompt_out, answer_out, dkv, dq_t, factors, scores, o_t
+    place,
+    q_t,
+    do_t,
+    both_s,
+    kv,
+    answer_kv,
+    o_in,
+    stats,
+    prompt_out,
+    answer_out,
+    dkv,
+    dq_t,
+    factors,
+    scores,
+    answer_scores,
+    o_t,
 ):
     rows = kv.shape[1]
     prompt, answer, every = sides(q_t)
@@ -195,11 +220,19 @@
     part = slice(0, rows)
     chunks = where.other_chunks
     run = score_pass(kv, part, q_t, every, where.other_limit, chunks, scores)
+    answer_run = score_pass(
+        answer_kv, part, q_t, answer, where.answer_limit, where.answer_chunks, answer_scores
+    )
+    run = jnp.concatenate([run[:, prompt], jnp.maximum(run[:, answer], answer_run)], axis=1)
     own_max = stats[0:1, :]
     row_max = jnp.maximum(jnp.max(run, axis=0, keepdims=True) * TO_LOG2, own_max)
     shrink = jnp.exp2(own_max - row_max)
     o_t[...] = o_in[...] * shrink
     total = value_pass(kv, part, every, row_max, chunks, scores, o_t) + stats[1:2, :] * shrink
+    answer_total = value_pass(
+        answer_kv, part, answer, row_max[:, answer], where.answer_chunks, answer_scores, o_t
+    )
+    total = jnp.concatenate([total[:, prompt], total[:, answer] + answer_total], axis=1)
     inverse = 1.0 / total
     out_t = o_t[...] * inverse
     delta = jnp.sum(do_t[...].astype(F32) * out_t, axis=0, keepdims=True)
@@ -211,7 +244,7 @@
 
     def step(c, _):
         shares = scores[at(c), :] * inverse
-        gradients(kv, c, part, shares, every, do_t, both_s, delta, dkv, dq_t)
+        gradients(kv, c, part, shares, every, do_t, both_s, delta, dkv, part, dq_t)
         return 0
 
     lax.fori_loop(0, chunks, step, 0)
@@ -219,27 +252,28 @@
 
 
 def own_backward_kernel(
-    place, q_t, do_t, both_s, kv, factors, dq_in, prompt_dq, answer_dq, dkv, dq_t
+    place, q_t, do_t, both_s, kv, answer_kv, factors, dq_in, prompt_dq, answer_dq, dkv, dq_t
 ):
-    rows = kv.shape[1] // 2
+    rows = kv.shape[1]
     prompt, answer, every = sides(q_t)
     where = Place(place, rows, kv.shape[0] * rows)
+    part = slice(0, rows)
     dq_t[...] = dq_in[...]
 
-    def run(part, side, limit, chunks):
+    def run(kv, out_part, side, limit, chunks):
         log_total, delta = factors[0:1, side], factors[1:2, side]
 
         def step(c, _):
             s = masked_scores(kv, c, part, q_t[:, side], limit)
             shares = jnp.exp2(s * TO_LOG2 - log_total)
-            gradients(kv, c, part, shares, side, do_t, both_s, delta, dkv, dq_t)
+            gradients(kv, c, part, shares, side, do_t, both_s, delta, dkv, out_part, dq_t)
             return 0
 
         lax.fori_loop(0, chunks, step, 0)
-        blank(dkv, part, chunks)
-
-    run(slice(0, rows), every, where.own_limit, where.own_chunks)
-    run(slice(rows, 2 * rows), answer, where.answer_limit, where.answer_chunks)
+        blank(dkv, out_part, chunks)
+
+    run(kv, part, every, where.own_limit, where.own_chunks)
+    run(answer_kv, slice(rows, 2 * rows), answer, where.answer_limit, where.answer_chunks)
     write_rows(prompt_dq, dq_t[:, prompt] * SCALING, rows)
     write_rows(answer_dq, dq_t[:, answer] * SCALING, rows)
 
@@ -257,30 +291,23 @@
     )(*arrays)
 
 
-def copies_of(parts, count):
-    rows = parts[0].shape[0]
-
-    def kernel(pk, pv, ak, av, out, alone):
-        alone[:, KEYS] = pk[...]
-        alone[:, VALUES] = pv[...]
+def copies_of(keys, values, count):
+    rows = keys.shape[0]
+
+    def kernel(k, v, out):
         for i in range(count):
-            out[i, :rows, KEYS] = pk[...]
-            out[i, :rows, VALUES] = pv[...]
-            out[i, rows:, KEYS] = ak[...]
-            out[i, rows:, VALUES] = av[...]
+            out[i, :, KEYS] = k[...]
+            out[i, :, VALUES] = v[...]
 
     return pl.pallas_call(
         kernel,
-        out_shape=[
-            jax.ShapeDtypeStruct((count, 2 * rows, 2 * HEAD_SIZE), BF16),
-            jax.ShapeDtypeStruct((rows, 2 * HEAD_SIZE), BF16),
-        ],
-        in_specs=[VMEM] * 4,
-        out_specs=[VMEM] * 2,
+        out_shape=jax.ShapeDtypeStruct((count, rows, 2 * HEAD_SIZE), BF16),
+        in_specs=[VMEM] * 2,
+        out_specs=VMEM,
         compiler_params=pltpu.CompilerParams(vmem_limit_bytes=67043328),
         cost_estimate=pl.CostEstimate(flops=10**6, bytes_accessed=0, transcendentals=0),
         name="copies",
-    )(*parts)
+    )(keys, values)
 
 
 def exchanged(pieces):
@@ -309,12 +336,7 @@
     pair_index = lax.axis_index("pair")
     count = lax.axis_size("ctx")
     half = count * rows
-    copies, alone = copies_of(
-        (prompt_key_rows, prompt_value_rows, response_key_rows[0], response_value_rows[0]), count
-    )
-    own_kv = exchanged(copies)
-    other = to_partner(alone)
-    other_copies = jnp.broadcast_to(other[None], (count, *other.shape))
+    own_kv = exchanged(copies_of(prompt_key_rows, prompt_value_rows, count))
     place = jnp.stack(
         [
             pair_index,
@@ -326,35 +348,45 @@
     wide, tall = (HEAD_SIZE, 2 * lanes), (2 * lanes, 2 * HEAD_SIZE)
     out = ((rows, GROUP * HEAD_SIZE), BF16)
     stat = ((8, 2 * lanes), F32)
-    q_t, do_t, both_s = call(
+    kv_shape = (count, rows, 2 * HEAD_SIZE)
+    q_t, do_t, both_s, answer_copies = call(
         lambda *refs: prepare_kernel(*refs, half=half),
         "prepare",
-        (place, prompt_queries, answer_queries[0], prompt_cotangent, answer_cotangent[0]),
-        [(wide, BF16), (wide, BF16), (tall, BF16)],
+        (
+            place,
+            prompt_queries,
+            answer_queries[0],
+            prompt_cotangent,
+            answer_cotangent[0],
+            response_key_rows[0],
+            response_value_rows[0],
+        ),
+        [(wide, BF16), (wide, BF16), (tall, BF16), (kv_shape, BF16)],
         [],
         10**9,
         8,
     )
-    own_kv, other_copies, q_t, do_t, both_s = lax.optimization_barrier(
-        (own_kv, other_copies, q_t, do_t, both_s)
-    )
-    other_kv = exchanged(other_copies)
+    own_kv, answer_copies, q_t, do_t, both_s = lax.optimization_barrier(
+        (own_kv, answer_copies, q_t, do_t, both_s)
+    )
+    other_kv = to_partner(own_kv)
+    answer_kv = exchanged(answer_copies)
     flops = 2 * half * lanes * HEAD_SIZE
     o_t, stats = call(
         own_forward_kernel,
         "own_forward",
         (place, q_t, own_kv),
         [(wide, F32), stat],
-        [((half, 2 * lanes), F32), ((half, lanes), F32)],
+        [((half, 2 * lanes), F32)],
         8 * flops,
         16,
     )
     prompt_out, answer_out, other_dkv, dq_t, factors = call(
         other_kernel,
         "other",
-        (place, q_t, do_t, both_s, other_kv, o_t, stats),
-        [out, out, (other_kv.shape, BF16), (wide, F32), stat],
-        [((half, 2 * lanes), F32), (wide, F32)],
+        (place, q_t, do_t, both_s, other_kv, answer_kv, o_t, stats),
+        [out, out, (kv_shape, BF16), (wide, F32), stat],
+        [((half, 2 * lanes), F32), ((half, lanes), F32), (wide, F32)],
         12 * flops,
         16,
     )
@@ -362,8 +394,8 @@
     prompt_dq, answer_dq, own_dkv = call(
         own_backward_kernel,
         "own_backward",
-        (place, q_t, do_t, both_s, own_kv, factors, dq_t),
-        [out, out, (own_kv.shape, BF16)],
+        (place, q_t, do_t, both_s, own_kv, answer_kv, factors, dq_t),
+        [out, out, ((count, 2 * rows, 2 * HEAD_SIZE), BF16)],
         [(wide, F32)],
         18 * flops,
         16,

time: 83.2 us -> 79.1 us (0.951)
  waiting for transfers between devices: 42.2 us -> 31.3 us
  Pallas kernels: 14.5 us -> 19.4 us
  starting transfers between devices: 19.3 us -> 21.5 us
    all_to_all x4, waiting for transfers between devices: 42 us -> 31.3 us  [exchanged(): lax.all_to_all(pieces, 'ctx', split_axis=0, concat_axis=0, tiled=True)]
    pallas_call x4, Pallas kernels: 12.6 us -> 17.8 us  [call(): pl.pallas_call(kernel, out_shape=[jax.ShapeDtypeStruct(*o) for o in outs]...]
    all_to_all x4, starting transfers between devices: 18.1 us -> 19.4 us  [exchanged(): lax.all_to_all(pieces, 'ctx', split_axis=0, concat_axis=0, tiled=True)]
    ppermute x2, starting transfers between devices: 1.19 us -> 2.11 us  [to_partner(): lax.ppermute(block, 'pair', [(i, count - 1 - i) for i in range(count)])]
    broadcast_in_dim x1 -> x0, local copies, waits for them, and re-layouts: 0.84 us -> none  [body(): other_copies = jnp.broadcast_to(other[None], (count, *other.shape))]
    unnamed x18 -> x20, local copies, waits for them, and re-layouts: 0.99 us -> 1.69 us
  transfers between devices with their start and end apart: 6 -> 6, of which waited for: 5 -> 4; matrix products, arithmetic and copies ran while one was open for 3% -> 3% of each run, Pallas kernels for 7% -> 13%
where the time goes in v2:
time: 79.1 us; the launch traced here: 78.1 us
  waiting for transfers between devices  31.3 us (40%)
  starting transfers between devices  21.5 us (27%)
  Pallas kernels  19.4 us (25%)
  local copies, waits for them, and re-layouts  3.51 us (4%)
  between operations  1.43 us (2%)
  other arithmetic  0.96 us (1%)
    all_to_all x4, waiting for transfers between devices, exchanged(): lax.all_to_all(pieces, 'ctx', split_axis=0, concat_axis=0, tiled=True)  31.3 us
    all_to_all x4, starting transfers between devices, exchanged(): lax.all_to_all(pieces, 'ctx', split_axis=0, concat_axis=0, tiled=True)  19.4 us
    pallas_call x4, Pallas kernels, call(): pl.pallas_call(kernel, out_shape=[jax.ShapeDtypeStruct(*o) for o in outs]...  17.8 us
    ppermute x2, starting transfers between devices, to_partner(): lax.ppermute(block, 'pair', [(i, count - 1 - i) for i in range(count)])  2.11 us
    unnamed x20, local copies, waits for them, and re-layouts  1.69 us
    pallas_call x1, Pallas kernels, copies_of(): pl.pallas_call(kernel, out_shape=jax.ShapeDtypeStruct((count, rows, 2 * H...  1.6 us
  transfers between devices with their start and end apart: 6, of which 4 were waited for; matrix products, arithmetic and copies ran while one was open for 3% of the time, Pallas kernels for 13%

profile of v2, /device:TPU:160, one launch (start us, length us, event | category | flops | bytes accessed | tf_op | source)
XLA Modules:
  0.0 78.1 jit_solution(16059796701321410391)
XLA Ops:
  0.6 1.6 %copies.1 = bf16[16,64,256]{2,1,0:T(8,128)(2,1)} custom-call(bf16[64,128]{1,0:T(8,128)(2,1)} %k.1, bf16[64,128]{1,0:T(8,128)(2,1)} %v.1), custom_call_target="tpu_custom_call" | custom-call | flops 1000000 | tf_op jit(solution)/shard_map/copies/pallas_call | solution.py:302
  2.2 0.0 copy-start.9
  2.2 0.0 copy-start
  2.2 0.0 copy-start.1
  2.2 0.0 copy-start.2
  2.2 0.0 copy-start.3
  2.3 0.0 copy-start.4
  2.3 0.0 copy-start.5
  2.3 7.2 %all-to-all-start = ((bf16[16,64,256]{2,1,0:T(8,128)(2,1)}), bf16[16,64,256]{2,1,0:T(8,128)(2,1)S(1)}, u32[]{:S(2)}, u32[]{:S(2)}) async-start(bf16[16,64,256]{2,1,0:T(8,128)(2,1)} %copies.1), calls=%async_computation | async-start | bytes 1048576 | tf_op jit(solution)/shard_map/all_to_all | solution.py:314
  10.1 0.0 copy-done.9
  10.1 0.6 dynamic_slice.4
  10.7 0.7 pad_add_fusion.refs_0_.place
  11.4 0.0 copy-done
  11.4 0.0 copy-done.1
  11.5 0.0 copy-done.2
  11.5 0.0 copy-done.3
  11.5 0.0 copy-done.4
  11.5 0.0 copy-done.5
  11.5 1.6 %prepare.1 = (bf16[128,1024]{1,0:T(8,128)(2,1)S(1)}, bf16[128,1024]{1,0:T(8,128)(2,1)S(1)}, bf16[1024,256]{1,0:T(8,128)(2,1)S(1)}, bf16[16,64,256]{2,1,0:T(8,128)(2,1)}) custom-call(s32[4]{0:T(128)S(1)} %pad_add_fusion.refs_0_.place, bf16[64,1024]{1,0:T(8,128)(2,1)S(1)} %copy-done, bf16[64,1024]{1,0:T(8,128)(2,1)S(1)} %bitcast.12, ...), custom_call_target="tpu_custom_call" | custom-call | flops 1000000000 | tf_op jit(solution)/shard_map/prepare/pallas_call | solution.py:282
  13.0 0.0 copy-start.6
  13.0 0.7 copy-done.6
  13.7 7.2 %all-to-all-done.kv = bf16[16,64,256]{2,1,0:T(8,128)(2,1)S(1)} async-done(((bf16[16,64,256]{2,1,0:T(8,128)(2,1)}), bf16[16,64,256]{2,1,0:T(8,128)(2,1)S(1)}, u32[]{:S(2)}, u32[]{:S(2)}) %all-to-all-start) | async-done | bytes 524320 | tf_op jit(solution)/shard_map/all_to_all | solution.py:314
  21.0 1.0 %collective-permute-start = (bf16[16,64,256]{2,1,0:T(8,128)(2,1)S(1)}, bf16[16,64,256]{2,1,0:T(8,128)(2,1)S(1)}, u32[]{:S(2)}, u32[]{:S(2)}) collective-permute-start(bf16[16,64,256]{2,1,0:T(8,128)(2,1)S(1)} %all-to-all-done.kv), channel_id=1, source_target_pairs={{0,128},{128,0},{1,129},{129,1},{2,130},{130,2},{3,131},{131,3},{4... | collective-permute-start | bytes 1572872 | tf_op jit(solution)/shard_map/ppermute | solution.py:319
  22.0 3.6 %all-to-all-start.1 = ((bf16[16,64,256]{2,1,0:T(8,128)(2,1)}), bf16[16,64,256]{2,1,0:T(8,128)(2,1)S(1)}, u32[]{:S(2)}, u32[]{:S(2)}) async-start(bf16[16,64,256]{2,1,0:T(8,128)(2,1)} %get-tuple-element.35), calls=%async_computation.1 | async-start | bytes 1048576 | tf_op jit(solution)/shard_map/all_to_all | solution.py:314
  25.5 3.1 %own_forward.1 = (f32[128,1024]{1,0:T(8,128)S(1)}, f32[8,1024]{1,0:T(8,128)S(1)}) custom-call(s32[4]{0:T(128)S(1)} %pad_add_fusion.refs_0_.place, bf16[128,1024]{1,0:T(8,128)(2,1)S(1)} %get-tuple-element.31.q_t, bf16[16,64,256]{2,1,0:T(8,128)(2,1)S(1)} %all-to-all-done.kv), custom_call_target="tpu_custom_call" | custom-call | flops 1073741824 | tf_op jit(solution)/shard_map/own_forward/pallas_call | solution.py:282
  28.7 6.9 %all-to-all-done.1.answer_kv = bf16[16,64,256]{2,1,0:T(8,128)(2,1)S(1)} async-done(((bf16[16,64,256]{2,1,0:T(8,128)(2,1)}), bf16[16,64,256]{2,1,0:T(8,128)(2,1)S(1)}, u32[]{:S(2)}, u32[]{:S(2)}) %all-to-all-start.1) | async-done | bytes 524320 | tf_op jit(solution)/shard_map/all_to_all | solution.py:314
  35.6 0.0 collective-permute-done.kv
  35.6 0.0 copy-start.7
  35.6 0.9 %copy-done.7 = bf16[128,1024]{1,0:T(8,128)(2,1)S(1)} copy-done((bf16[128,1024]{1,0:T(8,128)(2,1)S(1)}, bf16[128,1024]{1,0:T(8,128)(2,1)}, u32[]{:S(2)}) %copy-start.7) | copy-done | bytes 262168
  36.6 7.3 %other.1 = (bf16[64,1024]{1,0:T(8,128)(2,1)}, bf16[64,1024]{1,0:T(8,128)(2,1)}, bf16[16,64,256]{2,1,0:T(8,128)(2,1)}, f32[128,1024]{1,0:T(8,128)S(1)}, f32[8,1024]{1,0:T(8,128)S(1)}) custom-call(s32[4]{0:T(128)S(1)} %pad_add_fusion.refs_0_.place, bf16[128,1024]{1,0:T(8,128)(2,1)S(1)} %get-tuple-element.31.q_t, bf16[128,1024]{1,0:T(8,128)(2,1)S(1)} %copy-done.7, ...), custom_call_target="tpu_custom_call" | custom-call | flops 1610612736 | tf_op jit(solution)/shard_map/other/pallas_call | solution.py:282
  43.9 0.0 copy-start.8
  43.9 4.5 %all-to-all-start.3 = ((bf16[16,64,256]{2,1,0:T(8,128)(2,1)}), bf16[16,64,256]{2,1,0:T(8,128)(2,1)S(1)}, u32[]{:S(2)}, u32[]{:S(2)}) async-start(bf16[16,64,256]{2,1,0:T(8,128)(2,1)} %get-tuple-element.44), calls=%async_computation.3 | async-start | bytes 1048576 | tf_op jit(solution)/shard_map/all_to_all | solution.py:314
  48.4 0.0 copy-done.8
  48.4 5.8 %own_backward.1 = (bf16[64,1024]{1,0:T(8,128)(2,1)}, bf16[64,1024]{1,0:T(8,128)(2,1)}, bf16[16,128,256]{2,1,0:T(8,128)(2,1)}) custom-call(s32[4]{0:T(128)S(1)} %pad_add_fusion.refs_0_.place, bf16[128,1024]{1,0:T(8,128)(2,1)S(1)} %get-tuple-element.31.q_t, bf16[128,1024]{1,0:T(8,128)(2,1)S(1)} %copy-done.8, bf16[1024,256]{1,0:T(8,128)(2,1)S(1)} %get-tuple-element.33.both_s, ...), custom_call_target="tpu_custom_call" | custom-call | flops 2415919104 | tf_op jit(solution)/shard_map/own_backward/pallas_call | solution.py:282
  54.2 4.2 %all-to-all-done.3 = bf16[16,64,256]{2,1,0:T(8,128)(2,1)S(1)} async-done(((bf16[16,64,256]{2,1,0:T(8,128)(2,1)}), bf16[16,64,256]{2,1,0:T(8,128)(2,1)S(1)}, u32[]{:S(2)}, u32[]{:S(2)}) %all-to-all-start.3) | async-done | bytes 524320 | tf_op jit(solution)/shard_map/all_to_all | solution.py:314
  58.5 4.1 %all-to-all-start.2 = ((bf16[16,128,256]{2,1,0:T(8,128)(2,1)}), bf16[16,128,256]{2,1,0:T(8,128)(2,1)S(1)}, u32[]{:S(2)}, u32[]{:S(2)}) async-start(bf16[16,128,256]{2,1,0:T(8,128)(2,1)} %get-tuple-element.43), calls=%async_computation.2 | async-start | bytes 2097152 | tf_op jit(solution)/shard_map/all_to_all | solution.py:314
  62.6 0.1 convert_reduce_fusion.1
  62.7 1.1 %collective-permute-start.1 = (f32[64,256]{1,0:T(8,128)S(1)}, f32[64,256]{1,0:T(8,128)S(1)}, u32[]{:S(2)}, u32[]{:S(2)}) collective-permute-start(f32[64,256]{1,0:T(8,128)S(1)} %convert_reduce_fusion.1), channel_id=1, source_target_pairs={{0,128},{128,0},{1,129},{129,1},{2,130},{130,2},{3,131},{131,3},{4... | collective-permute-start | bytes 196616 | tf_op jit(solution)/shard_map/ppermute | solution.py:319
  63.8 12.9 %all-to-all-done.2 = bf16[16,128,256]{2,1,0:T(8,128)(2,1)S(1)} async-done(((bf16[16,128,256]{2,1,0:T(8,128)(2,1)}), bf16[16,128,256]{2,1,0:T(8,128)(2,1)S(1)}, u32[]{:S(2)}, u32[]{:S(2)}) %all-to-all-start.2) | async-done | bytes 1048608 | tf_op jit(solution)/shard_map/all_to_all | solution.py:314
  76.7 0.1 convert_reduce_fusion
  76.8 0.6 slice_bitcast_fusion
  77.4 0.0 collective-permute-done.1
  77.4 0.6 fusion.1
  (2 shorter events, 0.0 us)
Async XLA Ops:
  2.2 7.9 %copy-start.9 = (s32[2]{0:T(128)S(1)}, s32[2]{0:T(128)}, u32[]{:S(2)}) copy-start(s32[2]{0:T(128)} %param.19) | copy-start | bytes 28
  2.2 9.2 %copy-start = (bf16[64,1024]{1,0:T(8,128)(2,1)S(1)}, bf16[64,1024]{1,0:T(8,128)(2,1)}, u32[]{:S(2)}) copy-start(bf16[64,1024]{1,0:T(8,128)(2,1)} %refs_1_.1) | copy-start | bytes 393220
  2.2 9.2 %copy-start.1 = (bf16[1,64,1024]{2,1,0:T(8,128)(2,1)S(1)}, bf16[1,64,1024]{2,1,0:T(8,128)(2,1)}, u32[]{:S(2)}) copy-start(bf16[1,64,1024]{2,1,0:T(8,128)(2,1)} %param.13) | copy-start | bytes 393220
  2.2 9.2 %copy-start.2 = (bf16[64,1024]{1,0:T(8,128)(2,1)S(1)}, bf16[64,1024]{1,0:T(8,128)(2,1)}, u32[]{:S(2)}) copy-start(bf16[64,1024]{1,0:T(8,128)(2,1)} %refs_3_.1) | copy-start | bytes 393220
  2.2 9.2 %copy-start.3 = (bf16[1,64,1024]{2,1,0:T(8,128)(2,1)S(1)}, bf16[1,64,1024]{2,1,0:T(8,128)(2,1)}, u32[]{:S(2)}) copy-start(bf16[1,64,1024]{2,1,0:T(8,128)(2,1)} %param.17) | copy-start | bytes 393220
  2.3 9.2 %copy-start.4 = (bf16[1,64,128]{2,1,0:T(8,128)(2,1)S(1)}, bf16[1,64,128]{2,1,0:T(8,128)(2,1)}, u32[]{:S(2)}) copy-start(bf16[1,64,128]{2,1,0:T(8,128)(2,1)} %param.14) | copy-start | bytes 49156
  2.3 9.2 %copy-start.5 = (bf16[1,64,128]{2,1,0:T(8,128)(2,1)S(1)}, bf16[1,64,128]{2,1,0:T(8,128)(2,1)}, u32[]{:S(2)}) copy-start(bf16[1,64,128]{2,1,0:T(8,128)(2,1)} %param.15) | copy-start | bytes 49156
  2.3 18.7 %all-to-all-start = ((bf16[16,64,256]{2,1,0:T(8,128)(2,1)}), bf16[16,64,256]{2,1,0:T(8,128)(2,1)S(1)}, u32[]{:S(2)}, u32[]{:S(2)}) async-start(bf16[16,64,256]{2,1,0:T(8,128)(2,1)} %copies.1), calls=%async_computation | async-start | bytes 1048576 | tf_op jit(solution)/shard_map/all_to_all | solution.py:314
  13.0 0.7 copy-start.6
  21.0 14.6 %collective-permute-start = (bf16[16,64,256]{2,1,0:T(8,128)(2,1)S(1)}, bf16[16,64,256]{2,1,0:T(8,128)(2,1)S(1)}, u32[]{:S(2)}, u32[]{:S(2)}) collective-permute-start(bf16[16,64,256]{2,1,0:T(8,128)(2,1)S(1)} %all-to-all-done.kv), channel_id=1, source_target_pairs={{0,128},{128,0},{1,129},{129,1},{2,130},{130,2},{3,131},{131,3},{4... | collective-permute-start | bytes 1572872 | tf_op jit(solution)/shard_map/ppermute | solution.py:319
  22.0 13.6 %all-to-all-start.1 = ((bf16[16,64,256]{2,1,0:T(8,128)(2,1)}), bf16[16,64,256]{2,1,0:T(8,128)(2,1)S(1)}, u32[]{:S(2)}, u32[]{:S(2)}) async-start(bf16[16,64,256]{2,1,0:T(8,128)(2,1)} %get-tuple-element.35), calls=%async_computation.1 | async-start | bytes 1048576 | tf_op jit(solution)/shard_map/all_to_all | solution.py:314
  35.6 1.0 %copy-start.7 = (bf16[128,1024]{1,0:T(8,128)(2,1)S(1)}, bf16[128,1024]{1,0:T(8,128)(2,1)}, u32[]{:S(2)}) copy-start(bf16[128,1024]{1,0:T(8,128)(2,1)} %copy-done.6) | copy-start | bytes 786436
  43.9 4.5 %copy-start.8 = (bf16[128,1024]{1,0:T(8,128)(2,1)S(1)}, bf16[128,1024]{1,0:T(8,128)(2,1)}, u32[]{:S(2)}) copy-start(bf16[128,1024]{1,0:T(8,128)(2,1)} %copy-done.6) | copy-start | bytes 786436
  43.9 14.6 %all-to-all-start.3 = ((bf16[16,64,256]{2,1,0:T(8,128)(2,1)}), bf16[16,64,256]{2,1,0:T(8,128)(2,1)S(1)}, u32[]{:S(2)}, u32[]{:S(2)}) async-start(bf16[16,64,256]{2,1,0:T(8,128)(2,1)} %get-tuple-element.44), calls=%async_computation.3 | async-start | bytes 1048576 | tf_op jit(solution)/shard_map/all_to_all | solution.py:314
  58.5 18.2 %all-to-all-start.2 = ((bf16[16,128,256]{2,1,0:T(8,128)(2,1)}), bf16[16,128,256]{2,1,0:T(8,128)(2,1)S(1)}, u32[]{:S(2)}, u32[]{:S(2)}) async-start(bf16[16,128,256]{2,1,0:T(8,128)(2,1)} %get-tuple-element.43), calls=%async_computation.2 | async-start | bytes 2097152 | tf_op jit(solution)/shard_map/all_to_all | solution.py:314
  62.7 14.8 %collective-permute-start.1 = (f32[64,256]{1,0:T(8,128)S(1)}, f32[64,256]{1,0:T(8,128)S(1)}, u32[]{:S(2)}, u32[]{:S(2)}) collective-permute-start(f32[64,256]{1,0:T(8,128)S(1)} %convert_reduce_fusion.1), channel_id=1, source_target_pairs={{0,128},{128,0},{1,129},{129,1},{2,130},{130,2},{3,131},{131,3},{4... | collective-permute-start | bytes 196616 | tf_op jit(solution)/shard_map/ppermute | solution.py:319

commit v3 on v2

--- a/solution.py
+++ b/solution.py
@@ -69,7 +69,6 @@
     answer_k,
     answer_v,
     q_t,
-    do_t,
     both_s,
     answer_copies,
     *,
@@ -100,7 +99,6 @@
         both_s[side, KEYS] = q_rows
         both_s[side, VALUES] = do_rows
         q_t[:, side] = q_rows.T
-        do_t[:, side] = do_rows.T
 
 
 def block_of(kv, c, part, cols):
@@ -109,11 +107,11 @@
     return kv[pl.ds(c * count, count), part, cols].reshape(CHUNK, HEAD_SIZE)
 
 
-def put_block(dkv, c, part, dk, dv):
-    rows = part.stop - part.start
+def put_block(dkv, c, dk, dv):
+    rows = dkv.shape[1]
     count = CHUNK // rows
-    dkv[pl.ds(c * count, count), part, KEYS] = dk.astype(BF16).reshape(count, rows, HEAD_SIZE)
-    dkv[pl.ds(c * count, count), part, VALUES] = dv.astype(BF16).reshape(count, rows, HEAD_SIZE)
+    for cols, d in ((KEYS, dk), (VALUES, dv)):
+        dkv[pl.ds(c * count, count), :, cols] = d.astype(dkv.dtype).reshape(count, rows, HEAD_SIZE)
 
 
 def masked_scores(kv, c, part, q_t, limit):
@@ -147,26 +145,25 @@
     return jnp.sum(lax.fori_loop(0, chunks, step, start), axis=0, keepdims=True)
 
 
-def gradients(kv, c, part, shares, side, do_t, both_s, delta, dkv, out_part, dq_t):
+def gradients(kv, c, part, shares, side, do_t, both_s, delta, dkv, dq_t):
     dp = dot(block_of(kv, c, part, VALUES), do_t[:, side], 1, 0)
     ds = (shares * (dp - delta)).astype(BF16)
     put_block(
         dkv,
         c,
-        out_part,
         dot(ds, both_s[side, KEYS], 1, 0) * SCALING,
         dot(shares.astype(BF16), both_s[side, VALUES], 1, 0),
     )
     dq_t[:, side] += dot(block_of(kv, c, part, KEYS), ds, 0, 0)
 
 
-def blank(dkv, part, begin):
+def blank(dkv, begin):
     def step(c, _):
         zero = jnp.zeros((CHUNK, HEAD_SIZE), F32)
-        put_block(dkv, c, part, zero, zero)
+        put_block(dkv, c, zero, zero)
         return 0
 
-    lax.fori_loop(begin, dkv.shape[0] * (part.stop - part.start) // CHUNK, step, 0)
+    lax.fori_loop(begin, dkv.shape[0] * dkv.shape[1] // CHUNK, step, 0)
 
 
 def write_rows(ref, block_t, rows, first=None, length=None):
@@ -199,7 +196,6 @@
 def other_kernel(
     place,
     q_t,
-    do_t,
     both_s,
     kv,
     answer_kv,
@@ -208,11 +204,13 @@
     prompt_out,
     answer_out,
     dkv,
+    answer_dkv,
     dq_t,
     factors,
     scores,
     answer_scores,
     o_t,
+    do_t,
 ):
     rows = kv.shape[1]
     prompt, answer, every = sides(q_t)
@@ -224,6 +222,7 @@
         answer_kv, part, q_t, answer, where.answer_limit, where.answer_chunks, answer_scores
     )
     run = jnp.concatenate([run[:, prompt], jnp.maximum(run[:, answer], answer_run)], axis=1)
+    do_t[...] = both_s[:, VALUES].T
     own_max = stats[0:1, :]
     row_max = jnp.maximum(jnp.max(run, axis=0, keepdims=True) * TO_LOG2, own_max)
     shrink = jnp.exp2(own_max - row_max)
@@ -242,38 +241,39 @@
     write_rows(answer_out, out_t[:, answer], rows, where.first, where.answer_len)
     dq_t[...] = jnp.zeros_like(dq_t)
 
-    def step(c, _):
-        shares = scores[at(c), :] * inverse
-        gradients(kv, c, part, shares, every, do_t, both_s, delta, dkv, part, dq_t)
-        return 0
-
-    lax.fori_loop(0, chunks, step, 0)
-    blank(dkv, part, chunks)
+    def run(kv, scores, side, chunks, dkv):
+        def step(c, _):
+            shares = scores[at(c), :] * inverse[:, side]
+            gradients(kv, c, part, shares, side, do_t, both_s, delta[:, side], dkv, dq_t)
+            return 0
+
+        lax.fori_loop(0, chunks, step, 0)
+        blank(dkv, chunks)
+
+    run(kv, scores, every, chunks, dkv)
+    run(answer_kv, answer_scores, answer, where.answer_chunks, answer_dkv)
 
 
 def own_backward_kernel(
-    place, q_t, do_t, both_s, kv, answer_kv, factors, dq_in, prompt_dq, answer_dq, dkv, dq_t
+    place, both_s, kv, factors, dq_in, prompt_dq, answer_dq, dkv, dq_t, do_t, q_t
 ):
     rows = kv.shape[1]
     prompt, answer, every = sides(q_t)
     where = Place(place, rows, kv.shape[0] * rows)
     part = slice(0, rows)
+    do_t[...] = both_s[:, VALUES].T
+    q_t[...] = both_s[:, KEYS].T
     dq_t[...] = dq_in[...]
-
-    def run(kv, out_part, side, limit, chunks):
-        log_total, delta = factors[0:1, side], factors[1:2, side]
-
-        def step(c, _):
-            s = masked_scores(kv, c, part, q_t[:, side], limit)
-            shares = jnp.exp2(s * TO_LOG2 - log_total)
-            gradients(kv, c, part, shares, side, do_t, both_s, delta, dkv, out_part, dq_t)
-            return 0
-
-        lax.fori_loop(0, chunks, step, 0)
-        blank(dkv, out_part, chunks)
-
-    run(kv, part, every, where.own_limit, where.own_chunks)
-    run(answer_kv, slice(rows, 2 * rows), answer, where.answer_limit, where.answer_chunks)
+    log_total, delta = factors[0:1, :], factors[1:2, :]
+
+    def step(c, _):
+        s = masked_scores(kv, c, part, q_t[...], where.own_limit)
+        shares = jnp.exp2(s * TO_LOG2 - log_total)
+        gradients(kv, c, part, shares, every, do_t, both_s, delta, dkv, dq_t)
+        return 0
+
+    lax.fori_loop(0, where.own_chunks, step, 0)
+    blank(dkv, where.own_chunks)
     write_rows(prompt_dq, dq_t[:, prompt] * SCALING, rows)
     write_rows(answer_dq, dq_t[:, answer] * SCALING, rows)
 
@@ -349,7 +349,7 @@
     out = ((rows, GROUP * HEAD_SIZE), BF16)
     stat = ((8, 2 * lanes), F32)
     kv_shape = (count, rows, 2 * HEAD_SIZE)
-    q_t, do_t, both_s, answer_copies = call(
+    q_t, both_s, answer_copies = call(
         lambda *refs: prepare_kernel(*refs, half=half),
         "prepare",
         (
@@ -361,13 +361,13 @@
             response_key_rows[0],
             response_value_rows[0],
         ),
-        [(wide, BF16), (wide, BF16), (tall, BF16), (kv_shape, BF16)],
+        [(wide, BF16), (tall, BF16), (kv_shape, BF16)],
         [],
         10**9,
         8,
     )
-    own_kv, answer_copies, q_t, do_t, both_s = lax.optimization_barrier(
-        (own_kv, answer_copies, q_t, do_t, both_s)
+    own_kv, answer_copies, q_t, both_s = lax.optimization_barrier(
+        (own_kv, answer_copies, q_t, both_s)
     )
     other_kv = to_partner(own_kv)
     answer_kv = exchanged(answer_copies)
@@ -381,29 +381,28 @@
         8 * flops,
         16,
     )
-    prompt_out, answer_out, other_dkv, dq_t, factors = call(
+    prompt_out, answer_out, other_dkv, answer_dkv, dq_t, factors = call(
         other_kernel,
         "other",
-        (place, q_t, do_t, both_s, other_kv, answer_kv, o_t, stats),
-        [out, out, (kv_shape, BF16), (wide, F32), stat],
-        [((half, 2 * lanes), F32), ((half, lanes), F32), (wide, F32)],
-        12 * flops,
+        (place, q_t, both_s, other_kv, answer_kv, o_t, stats),
+        [out, out, (kv_shape, BF16), (kv_shape, BF16), (wide, F32), stat],
+        [((half, 2 * lanes), F32), ((half, lanes), F32), (wide, F32), (wide, BF16)],
+        16 * flops,
         16,
     )
-    other_sum = exchanged(other_dkv).astype(F32).sum(axis=0)
+    from_partner = to_partner(other_dkv)
+    answer_grad = exchanged(answer_dkv).astype(F32).sum(axis=0).astype(BF16)
     prompt_dq, answer_dq, own_dkv = call(
         own_backward_kernel,
         "own_backward",
-        (place, q_t, do_t, both_s, own_kv, answer_kv, factors, dq_t),
-        [out, out, ((count, 2 * rows, 2 * HEAD_SIZE), BF16)],
-        [(wide, F32)],
-        18 * flops,
+        (place, both_s, own_kv, factors, dq_t),
+        [out, out, (kv_shape, F32)],
+        [(wide, F32), (wide, BF16), (wide, BF16)],
+        12 * flops,
         16,
     )
-    from_partner = to_partner(other_sum)
-    own_sum = exchanged(own_dkv).astype(F32).sum(axis=0)
-    prompt_grad = (own_sum[:rows] + from_partner).astype(BF16)
-    answer_grad = own_sum[rows:].astype(BF16)
+    prompt_dkv = (own_dkv + from_partner.astype(F32)).astype(BF16)
+    prompt_grad = exchanged(prompt_dkv).astype(F32).sum(axis=0).astype(BF16)
     return (
         prompt_out,
         answer_out[None],

time: 79.1 us -> 76.1 us (0.962)
  waiting for transfers between devices: 31.3 us -> 28.5 us
  other arithmetic: 0.96 us -> 1.84 us
  local copies, waits for them, and re-layouts: 3.51 us -> 2.65 us
    all_to_all x4, waiting for transfers between devices: 31.3 us -> 28.5 us  [exchanged(): lax.all_to_all(pieces, 'ctx', split_axis=0, concat_axis=0, tiled=True)]
    convert_element_type x1, other arithmetic: 0.01 us -> 0.97 us  [body(): prompt_dkv = (own_dkv + from_partner.astype(F32)).astype(BF16)]
    unnamed x20 -> x18, local copies, waits for them, and re-layouts: 1.69 us -> 0.83 us
    all_to_all x4, starting transfers between devices: 19.4 us -> 20.2 us  [exchanged(): lax.all_to_all(pieces, 'ctx', split_axis=0, concat_axis=0, tiled=True)]
  transfers between devices with their start and end apart: 6 -> 6, of which waited for: 4 -> 4; matrix products, arithmetic and copies ran while one was open for 3% -> 4% of each run, Pallas kernels for 13% -> 13%
where the time goes in v3:
time: 76.1 us; the launch traced here: 75.6 us
  waiting for transfers between devices  28.5 us (37%)
  starting transfers between devices  22.2 us (29%)
  Pallas kernels  19 us (25%)
  local copies, waits for them, and re-layouts  2.65 us (3%)
  other arithmetic  1.84 us (2%)
  between operations  1.43 us (2%)
    all_to_all x4, waiting for transfers between devices, exchanged(): lax.all_to_all(pieces, 'ctx', split_axis=0, concat_axis=0, tiled=True)  28.5 us
    all_to_all x4, starting transfers between devices, exchanged(): lax.all_to_all(pieces, 'ctx', split_axis=0, concat_axis=0, tiled=True)  20.2 us
    pallas_call x4, Pallas kernels, call(): pl.pallas_call(kernel, out_shape=[jax.ShapeDtypeStruct(*o) for o in outs]...  17.4 us
    ppermute x2, starting transfers between devices, to_partner(): lax.ppermute(block, 'pair', [(i, count - 1 - i) for i in range(count)])  2.02 us
    pallas_call x1, Pallas kernels, copies_of(): pl.pallas_call(kernel, out_shape=jax.ShapeDtypeStruct((count, rows, 2 * H...  1.6 us
  transfers between devices with their start and end apart: 6, of which 4 were waited for; matrix products, arithmetic and copies ran while one was open for 4% of the time, Pallas kernels for 13%

profile of v3, /device:TPU:160, one launch (start us, length us, event | category | flops | bytes accessed | tf_op | source)
XLA Modules:
  0.0 75.6 jit_solution(3947918594539592745)
XLA Ops:
  0.6 1.6 %copies.1 = bf16[16,64,256]{2,1,0:T(8,128)(2,1)} custom-call(bf16[64,128]{1,0:T(8,128)(2,1)} %k.1, bf16[64,128]{1,0:T(8,128)(2,1)} %v.1), custom_call_target="tpu_custom_call" | custom-call | flops 1000000 | tf_op jit(solution)/shard_map/copies/pallas_call | solution.py:302
  2.2 0.0 copy-start.8
  2.2 0.0 copy-start
  2.2 0.0 copy-start.1
  2.2 0.0 copy-start.2
  2.3 0.0 copy-start.3
  2.3 7.2 %all-to-all-start = ((bf16[16,64,256]{2,1,0:T(8,128)(2,1)}), bf16[16,64,256]{2,1,0:T(8,128)(2,1)S(1)}, u32[]{:S(2)}, u32[]{:S(2)}) async-start(bf16[16,64,256]{2,1,0:T(8,128)(2,1)} %copies.1), calls=%async_computation | async-start | bytes 1048576 | tf_op jit(solution)/shard_map/all_to_all | solution.py:314
  9.5 0.0 copy-start.4
  9.5 0.0 copy-start.5
  10.1 0.0 copy-done.8
  10.1 0.6 dynamic_slice.4
  10.7 0.7 pad_add_fusion.refs_0_.place
  11.5 0.0 copy-done
  11.5 0.0 copy-done.1
  11.5 0.0 copy-done.2
  11.5 0.0 copy-done.3
  11.5 0.0 copy-done.4
  11.5 0.0 copy-done.5
  11.5 1.5 %prepare.1 = (bf16[128,1024]{1,0:T(8,128)(2,1)S(1)}, bf16[1024,256]{1,0:T(8,128)(2,1)S(1)}, bf16[16,64,256]{2,1,0:T(8,128)(2,1)}) custom-call(s32[4]{0:T(128)S(1)} %pad_add_fusion.refs_0_.place, bf16[64,1024]{1,0:T(8,128)(2,1)S(1)} %copy-done, bf16[64,1024]{1,0:T(8,128)(2,1)S(1)} %bitcast.12, bf16[64,1024]{1,0:T(8,128)(2,1)S(1)} %copy-done.2, ...), custom_call_target="tpu_custom_call" | custom-call | flops 1000000000 | tf_op jit(solution)/shard_map/prepare/pallas_call | solution.py:282
  13.0 8.0 %all-to-all-done.kv = bf16[16,64,256]{2,1,0:T(8,128)(2,1)S(1)} async-done(((bf16[16,64,256]{2,1,0:T(8,128)(2,1)}), bf16[16,64,256]{2,1,0:T(8,128)(2,1)S(1)}, u32[]{:S(2)}, u32[]{:S(2)}) %all-to-all-start) | async-done | bytes 524320 | tf_op jit(solution)/shard_map/all_to_all | solution.py:314
  20.9 1.0 %collective-permute-start = (bf16[16,64,256]{2,1,0:T(8,128)(2,1)S(1)}, bf16[16,64,256]{2,1,0:T(8,128)(2,1)S(1)}, u32[]{:S(2)}, u32[]{:S(2)}) collective-permute-start(bf16[16,64,256]{2,1,0:T(8,128)(2,1)S(1)} %all-to-all-done.kv), channel_id=1, source_target_pairs={{0,128},{128,0},{1,129},{129,1},{2,130},{130,2},{3,131},{131,3},{4... | collective-permute-start | bytes 1572872 | tf_op jit(solution)/shard_map/ppermute | solution.py:319
  21.9 3.6 %all-to-all-start.1 = ((bf16[16,64,256]{2,1,0:T(8,128)(2,1)}), bf16[16,64,256]{2,1,0:T(8,128)(2,1)S(1)}, u32[]{:S(2)}, u32[]{:S(2)}) async-start(bf16[16,64,256]{2,1,0:T(8,128)(2,1)} %get-tuple-element.32), calls=%async_computation.1 | async-start | bytes 1048576 | tf_op jit(solution)/shard_map/all_to_all | solution.py:314
  25.5 3.1 %own_forward.1 = (f32[128,1024]{1,0:T(8,128)S(1)}, f32[8,1024]{1,0:T(8,128)S(1)}) custom-call(s32[4]{0:T(128)S(1)} %pad_add_fusion.refs_0_.place, bf16[128,1024]{1,0:T(8,128)(2,1)S(1)} %get-tuple-element.29.q_t, bf16[16,64,256]{2,1,0:T(8,128)(2,1)S(1)} %all-to-all-done.kv), custom_call_target="tpu_custom_call" | custom-call | flops 1073741824 | tf_op jit(solution)/shard_map/own_forward/pallas_call | solution.py:282
  28.6 6.9 %all-to-all-done.1.answer_kv = bf16[16,64,256]{2,1,0:T(8,128)(2,1)S(1)} async-done(((bf16[16,64,256]{2,1,0:T(8,128)(2,1)}), bf16[16,64,256]{2,1,0:T(8,128)(2,1)S(1)}, u32[]{:S(2)}, u32[]{:S(2)}) %all-to-all-start.1) | async-done | bytes 524320 | tf_op jit(solution)/shard_map/all_to_all | solution.py:314
  35.6 0.0 collective-permute-done.kv
  35.6 7.9 %other.1 = (bf16[64,1024]{1,0:T(8,128)(2,1)}, bf16[64,1024]{1,0:T(8,128)(2,1)}, bf16[16,64,256]{2,1,0:T(8,128)(2,1)S(1)}, bf16[16,64,256]{2,1,0:T(8,128)(2,1)}, ...) custom-call(s32[4]{0:T(128)S(1)} %pad_add_fusion.refs_0_.place, bf16[128,1024]{1,0:T(8,128)(2,1)S(1)} %get-tuple-element.29.q_t, ...), custom_call_target="tpu_custom_call" | custom-call | flops 2147483648 | tf_op jit(solution)/shard_map/other/pallas_call | solution.py:282
  43.5 0.0 copy-start.6
  43.5 0.8 %copy-done.6 = f32[128,1024]{1,0:T(8,128)} copy-done((f32[128,1024]{1,0:T(8,128)}, f32[128,1024]{1,0:T(8,128)S(1)}, u32[]{:S(2)}) %copy-start.6) | copy-done | bytes 524312
  44.3 1.0 %collective-permute-start.1 = (bf16[16,64,256]{2,1,0:T(8,128)(2,1)S(1)}, bf16[16,64,256]{2,1,0:T(8,128)(2,1)S(1)}, u32[]{:S(2)}, u32[]{:S(2)}) collective-permute-start(bf16[16,64,256]{2,1,0:T(8,128)(2,1)S(1)} %get-tuple-element.41), channel_id=1, source_target_pairs={{0,128},{128,0},{1,129},{129,1},{2,130},{130,2},{3,131},{131,3},{4... | collective-permute-start | bytes 1572872 | tf_op jit(solution)/shard_map/ppermute | solution.py:319
  45.3 0.0 copy-start.7
  45.3 5.9 %all-to-all-start.3 = ((bf16[16,64,256]{2,1,0:T(8,128)(2,1)}), bf16[16,64,256]{2,1,0:T(8,128)(2,1)S(1)}, u32[]{:S(2)}, u32[]{:S(2)}) async-start(bf16[16,64,256]{2,1,0:T(8,128)(2,1)} %get-tuple-element.43), calls=%async_computation.3 | async-start | bytes 1048576 | tf_op jit(solution)/shard_map/all_to_all | solution.py:314
  51.2 0.0 copy-done.7
  51.2 4.9 %own_backward.1 = (bf16[64,1024]{1,0:T(8,128)(2,1)}, bf16[64,1024]{1,0:T(8,128)(2,1)}, f32[16,64,256]{2,1,0:T(8,128)S(1)}) custom-call(s32[4]{0:T(128)S(1)} %pad_add_fusion.refs_0_.place, bf16[1024,256]{1,0:T(8,128)(2,1)S(1)} %get-tuple-element.30.both_s, bf16[16,64,256]{2,1,0:T(8,128)(2,1)S(1)} %all-to-all-done.kv, ...), custom_call_target="tpu_custom_call" | custom-call | flops 1610612736 | tf_op jit(solution)/shard_map/own_backward/pallas_call | solution.py:282
  56.1 0.0 collective-permute-done.1
  56.1 1.0 %add_convert_fusion = bf16[16,64,256]{2,1,0:T(8,128)(2,1)} fusion(f32[16,64,256]{2,1,0:T(8,128)S(1)} %get-tuple-element.40, bf16[16,64,256]{2,1,0:T(8,128)(2,1)S(1)} %collective-permute-done.1), kind=kLoop, calls=%fused_computation | loop fusion | flops 786432 | bytes 2097152 | tf_op jit(solution)/shard_map/convert_element_type | solution.py:404
  57.1 4.2 %all-to-all-done.3 = bf16[16,64,256]{2,1,0:T(8,128)(2,1)S(1)} async-done(((bf16[16,64,256]{2,1,0:T(8,128)(2,1)}), bf16[16,64,256]{2,1,0:T(8,128)(2,1)S(1)}, u32[]{:S(2)}, u32[]{:S(2)}) %all-to-all-start.3) | async-done | bytes 524320 | tf_op jit(solution)/shard_map/all_to_all | solution.py:314
  61.3 3.6 %all-to-all-start.2 = ((bf16[16,64,256]{2,1,0:T(8,128)(2,1)}), bf16[16,64,256]{2,1,0:T(8,128)(2,1)S(1)}, u32[]{:S(2)}, u32[]{:S(2)}) async-start(bf16[16,64,256]{2,1,0:T(8,128)(2,1)} %add_convert_fusion), calls=%async_computation.2 | async-start | bytes 1048576 | tf_op jit(solution)/shard_map/all_to_all | solution.py:314
  64.8 0.1 reduce_sum.25
  64.9 0.6 slice_bitcast_fusion
  65.5 9.4 %all-to-all-done.2 = bf16[16,64,256]{2,1,0:T(8,128)(2,1)S(1)} async-done(((bf16[16,64,256]{2,1,0:T(8,128)(2,1)}), bf16[16,64,256]{2,1,0:T(8,128)(2,1)S(1)}, u32[]{:S(2)}, u32[]{:S(2)}) %all-to-all-start.2) | async-done | bytes 524320 | tf_op jit(solution)/shard_map/all_to_all | solution.py:314
  74.9 0.1 reduce_sum.24
  75.0 0.6 fusion
Async XLA Ops:
  2.2 7.9 %copy-start.8 = (s32[2]{0:T(128)S(1)}, s32[2]{0:T(128)}, u32[]{:S(2)}) copy-start(s32[2]{0:T(128)} %param.19) | copy-start | bytes 28
  2.2 9.2 %copy-start = (bf16[64,1024]{1,0:T(8,128)(2,1)S(1)}, bf16[64,1024]{1,0:T(8,128)(2,1)}, u32[]{:S(2)}) copy-start(bf16[64,1024]{1,0:T(8,128)(2,1)} %refs_1_.1) | copy-start | bytes 393220
  2.2 9.2 %copy-start.1 = (bf16[1,64,1024]{2,1,0:T(8,128)(2,1)S(1)}, bf16[1,64,1024]{2,1,0:T(8,128)(2,1)}, u32[]{:S(2)}) copy-start(bf16[1,64,1024]{2,1,0:T(8,128)(2,1)} %param.13) | copy-start | bytes 393220
  2.2 9.2 %copy-start.2 = (bf16[64,1024]{1,0:T(8,128)(2,1)S(1)}, bf16[64,1024]{1,0:T(8,128)(2,1)}, u32[]{:S(2)}) copy-start(bf16[64,1024]{1,0:T(8,128)(2,1)} %refs_3_.1) | copy-start | bytes 393220
  2.3 9.2 %copy-start.3 = (bf16[1,64,1024]{2,1,0:T(8,128)(2,1)S(1)}, bf16[1,64,1024]{2,1,0:T(8,128)(2,1)}, u32[]{:S(2)}) copy-start(bf16[1,64,1024]{2,1,0:T(8,128)(2,1)} %param.17) | copy-start | bytes 393220
  2.3 18.7 %all-to-all-start = ((bf16[16,64,256]{2,1,0:T(8,128)(2,1)}), bf16[16,64,256]{2,1,0:T(8,128)(2,1)S(1)}, u32[]{:S(2)}, u32[]{:S(2)}) async-start(bf16[16,64,256]{2,1,0:T(8,128)(2,1)} %copies.1), calls=%async_computation | async-start | bytes 1048576 | tf_op jit(solution)/shard_map/all_to_all | solution.py:314
  9.5 2.0 %copy-start.4 = (bf16[1,64,128]{2,1,0:T(8,128)(2,1)S(1)}, bf16[1,64,128]{2,1,0:T(8,128)(2,1)}, u32[]{:S(2)}) copy-start(bf16[1,64,128]{2,1,0:T(8,128)(2,1)} %param.14) | copy-start | bytes 49156
  9.5 2.0 %copy-start.5 = (bf16[1,64,128]{2,1,0:T(8,128)(2,1)S(1)}, bf16[1,64,128]{2,1,0:T(8,128)(2,1)}, u32[]{:S(2)}) copy-start(bf16[1,64,128]{2,1,0:T(8,128)(2,1)} %param.15) | copy-start | bytes 49156
  20.9 14.6 %collective-permute-start = (bf16[16,64,256]{2,1,0:T(8,128)(2,1)S(1)}, bf16[16,64,256]{2,1,0:T(8,128)(2,1)S(1)}, u32[]{:S(2)}, u32[]{:S(2)}) collective-permute-start(bf16[16,64,256]{2,1,0:T(8,128)(2,1)S(1)} %all-to-all-done.kv), channel_id=1, source_target_pairs={{0,128},{128,0},{1,129},{129,1},{2,130},{130,2},{3,131},{131,3},{4... | collective-permute-start | bytes 1572872 | tf_op jit(solution)/shard_map/ppermute | solution.py:319
  21.9 13.6 %all-to-all-start.1 = ((bf16[16,64,256]{2,1,0:T(8,128)(2,1)}), bf16[16,64,256]{2,1,0:T(8,128)(2,1)S(1)}, u32[]{:S(2)}, u32[]{:S(2)}) async-start(bf16[16,64,256]{2,1,0:T(8,128)(2,1)} %get-tuple-element.32), calls=%async_computation.1 | async-start | bytes 1048576 | tf_op jit(solution)/shard_map/all_to_all | solution.py:314
  43.5 0.8 %copy-start.6 = (f32[128,1024]{1,0:T(8,128)}, f32[128,1024]{1,0:T(8,128)S(1)}, u32[]{:S(2)}) copy-start(f32[128,1024]{1,0:T(8,128)S(1)} %get-tuple-element.38.dq_in) | copy-start | bytes 1572868
  44.3 11.8 %collective-permute-start.1 = (bf16[16,64,256]{2,1,0:T(8,128)(2,1)S(1)}, bf16[16,64,256]{2,1,0:T(8,128)(2,1)S(1)}, u32[]{:S(2)}, u32[]{:S(2)}) collective-permute-start(bf16[16,64,256]{2,1,0:T(8,128)(2,1)S(1)} %get-tuple-element.41), channel_id=1, source_target_pairs={{0,128},{128,0},{1,129},{129,1},{2,130},{130,2},{3,131},{131,3},{4... | collective-permute-start | bytes 1572872 | tf_op jit(solution)/shard_map/ppermute | solution.py:319
  45.3 5.9 %copy-start.7 = (f32[128,1024]{1,0:T(8,128)S(1)}, f32[128,1024]{1,0:T(8,128)}, u32[]{:S(2)}) copy-start(f32[128,1024]{1,0:T(8,128)} %copy-done.6) | copy-start | bytes 1572868
  45.3 16.0 %all-to-all-start.3 = ((bf16[16,64,256]{2,1,0:T(8,128)(2,1)}), bf16[16,64,256]{2,1,0:T(8,128)(2,1)S(1)}, u32[]{:S(2)}, u32[]{:S(2)}) async-start(bf16[16,64,256]{2,1,0:T(8,128)(2,1)} %get-tuple-element.43), calls=%async_computation.3 | async-start | bytes 1048576 | tf_op jit(solution)/shard_map/all_to_all | solution.py:314
  61.3 13.6 %all-to-all-start.2 = ((bf16[16,64,256]{2,1,0:T(8,128)(2,1)}), bf16[16,64,256]{2,1,0:T(8,128)(2,1)S(1)}, u32[]{:S(2)}, u32[]{:S(2)}) async-start(bf16[16,64,256]{2,1,0:T(8,128)(2,1)} %add_convert_fusion), calls=%async_computation.2 | async-start | bytes 1048576 | tf_op jit(solution)/shard_map/all_to_all | solution.py:314

commit v4 on v3

--- a/solution.py
+++ b/solution.py
@@ -13,7 +13,7 @@
 SCALING = HEAD_SIZE ** (-0.5)
 LOG2E = 1.4426950408889634
 TO_LOG2 = SCALING * LOG2E
-CHUNK = 256
+CHUNK = 512
 F32 = jnp.float32
 BF16 = jnp.bfloat16
 VMEM = pl.BlockSpec(memory_space=pltpu.VMEM)

time: 76.1 us -> 74.3 us (0.976)
  Pallas kernels: 19 us -> 17.6 us
  starting transfers between devices: 22.2 us -> 21.2 us
  waiting for transfers between devices: 28.5 us -> 29.3 us
    pallas_call x4, Pallas kernels: 17.4 us -> 16 us  [call(): pl.pallas_call(kernel, out_shape=[jax.ShapeDtypeStruct(*o) for o in outs]...]
    all_to_all x4, starting transfers between devices: 20.2 us -> 19.2 us  [exchanged(): lax.all_to_all(pieces, 'ctx', split_axis=0, concat_axis=0, tiled=True)]
  transfers between devices with their start and end apart: 6 -> 6, of which waited for: 4 -> 5; matrix products, arithmetic and copies ran while one was open for 4% -> 4% of each run, Pallas kernels for 13% -> 12%
where the time goes in v4:
time: 74.3 us; the launch traced here: 74 us
  waiting for transfers between devices  29.3 us (39%)
  starting transfers between devices  21.2 us (29%)
  Pallas kernels  17.6 us (24%)
  local copies, waits for them, and re-layouts  2.65 us (4%)
  other arithmetic  1.84 us (2%)
  between operations  1.43 us (2%)
    all_to_all x4, waiting for transfers between devices, exchanged(): lax.all_to_all(pieces, 'ctx', split_axis=0, concat_axis=0, tiled=True)  28.7 us
    all_to_all x4, starting transfers between devices, exchanged(): lax.all_to_all(pieces, 'ctx', split_axis=0, concat_axis=0, tiled=True)  19.2 us
    pallas_call x4, Pallas kernels, call(): pl.pallas_call(kernel, out_shape=[jax.ShapeDtypeStruct(*o) for o in outs]...  16 us
    ppermute x2, starting transfers between devices, to_partner(): lax.ppermute(block, 'pair', [(i, count - 1 - i) for i in range(count)])  2.02 us
    pallas_call x1, Pallas kernels, copies_of(): pl.pallas_call(kernel, out_shape=jax.ShapeDtypeStruct((count, rows, 2 * H...  1.6 us
  transfers between devices with their start and end apart: 6, of which 5 were waited for; matrix products, arithmetic and copies ran while one was open for 4% of the time, Pallas kernels for 12%

profile of v4, /device:TPU:160, one launch (start us, length us, event | category | flops | bytes accessed | tf_op | source)
XLA Modules:
  0.0 74.0 jit_solution(17986531264889783210)
XLA Ops:
  0.6 1.6 %copies.1 = bf16[16,64,256]{2,1,0:T(8,128)(2,1)} custom-call(bf16[64,128]{1,0:T(8,128)(2,1)} %k.1, bf16[64,128]{1,0:T(8,128)(2,1)} %v.1), custom_call_target="tpu_custom_call" | custom-call | flops 1000000 | tf_op jit(solution)/shard_map/copies/pallas_call | solution.py:302
  2.2 0.0 copy-start.8
  2.2 0.0 copy-start
  2.2 0.0 copy-start.1
  2.2 0.0 copy-start.2
  2.3 0.0 copy-start.3
  2.3 7.2 %all-to-all-start = ((bf16[16,64,256]{2,1,0:T(8,128)(2,1)}), bf16[16,64,256]{2,1,0:T(8,128)(2,1)S(1)}, u32[]{:S(2)}, u32[]{:S(2)}) async-start(bf16[16,64,256]{2,1,0:T(8,128)(2,1)} %copies.1), calls=%async_computation | async-start | bytes 1048576 | tf_op jit(solution)/shard_map/all_to_all | solution.py:314
  9.5 0.0 copy-start.4
  9.5 0.0 copy-start.5
  10.1 0.0 copy-done.8
  10.1 0.6 dynamic_slice.4
  10.7 0.7 pad_add_fusion.refs_0_.place
  11.5 0.0 copy-done
  11.5 0.0 copy-done.1
  11.5 0.0 copy-done.2
  11.5 0.0 copy-done.3
  11.5 0.0 copy-done.4
  11.5 0.0 copy-done.5
  11.5 1.5 %prepare.1 = (bf16[128,1024]{1,0:T(8,128)(2,1)S(1)}, bf16[1024,256]{1,0:T(8,128)(2,1)S(1)}, bf16[16,64,256]{2,1,0:T(8,128)(2,1)}) custom-call(s32[4]{0:T(128)S(1)} %pad_add_fusion.refs_0_.place, bf16[64,1024]{1,0:T(8,128)(2,1)S(1)} %copy-done, bf16[64,1024]{1,0:T(8,128)(2,1)S(1)} %bitcast.12, bf16[64,1024]{1,0:T(8,128)(2,1)S(1)} %copy-done.2, ...), custom_call_target="tpu_custom_call" | custom-call | flops 1000000000 | tf_op jit(solution)/shard_map/prepare/pallas_call | solution.py:282
  13.0 8.0 %all-to-all-done.kv = bf16[16,64,256]{2,1,0:T(8,128)(2,1)S(1)} async-done(((bf16[16,64,256]{2,1,0:T(8,128)(2,1)}), bf16[16,64,256]{2,1,0:T(8,128)(2,1)S(1)}, u32[]{:S(2)}, u32[]{:S(2)}) %all-to-all-start) | async-done | bytes 524320 | tf_op jit(solution)/shard_map/all_to_all | solution.py:314
  20.9 1.0 %collective-permute-start = (bf16[16,64,256]{2,1,0:T(8,128)(2,1)S(1)}, bf16[16,64,256]{2,1,0:T(8,128)(2,1)S(1)}, u32[]{:S(2)}, u32[]{:S(2)}) collective-permute-start(bf16[16,64,256]{2,1,0:T(8,128)(2,1)S(1)} %all-to-all-done.kv), channel_id=1, source_target_pairs={{0,128},{128,0},{1,129},{129,1},{2,130},{130,2},{3,131},{131,3},{4... | collective-permute-start | bytes 1572872 | tf_op jit(solution)/shard_map/ppermute | solution.py:319
  21.9 3.6 %all-to-all-start.1 = ((bf16[16,64,256]{2,1,0:T(8,128)(2,1)}), bf16[16,64,256]{2,1,0:T(8,128)(2,1)S(1)}, u32[]{:S(2)}, u32[]{:S(2)}) async-start(bf16[16,64,256]{2,1,0:T(8,128)(2,1)} %get-tuple-element.32), calls=%async_computation.1 | async-start | bytes 1048576 | tf_op jit(solution)/shard_map/all_to_all | solution.py:314
  25.5 2.6 %own_forward.1 = (f32[128,1024]{1,0:T(8,128)S(1)}, f32[8,1024]{1,0:T(8,128)S(1)}) custom-call(s32[4]{0:T(128)S(1)} %pad_add_fusion.refs_0_.place, bf16[128,1024]{1,0:T(8,128)(2,1)S(1)} %get-tuple-element.29.q_t, bf16[16,64,256]{2,1,0:T(8,128)(2,1)S(1)} %all-to-all-done.kv), custom_call_target="tpu_custom_call" | custom-call | flops 1073741824 | tf_op jit(solution)/shard_map/own_forward/pallas_call | solution.py:282
  28.1 7.5 %all-to-all-done.1.answer_kv = bf16[16,64,256]{2,1,0:T(8,128)(2,1)S(1)} async-done(((bf16[16,64,256]{2,1,0:T(8,128)(2,1)}), bf16[16,64,256]{2,1,0:T(8,128)(2,1)S(1)}, u32[]{:S(2)}, u32[]{:S(2)}) %all-to-all-start.1) | async-done | bytes 524320 | tf_op jit(solution)/shard_map/all_to_all | solution.py:314
  35.6 0.0 collective-permute-done.kv
  35.6 7.3 %other.1 = (bf16[64,1024]{1,0:T(8,128)(2,1)}, bf16[64,1024]{1,0:T(8,128)(2,1)}, bf16[16,64,256]{2,1,0:T(8,128)(2,1)S(1)}, bf16[16,64,256]{2,1,0:T(8,128)(2,1)}, ...) custom-call(s32[4]{0:T(128)S(1)} %pad_add_fusion.refs_0_.place, bf16[128,1024]{1,0:T(8,128)(2,1)S(1)} %get-tuple-element.29.q_t, ...), custom_call_target="tpu_custom_call" | custom-call | flops 2147483648 | tf_op jit(solution)/shard_map/other/pallas_call | solution.py:282
  42.9 0.0 copy-start.6
  42.9 0.8 %copy-done.6 = f32[128,1024]{1,0:T(8,128)} copy-done((f32[128,1024]{1,0:T(8,128)}, f32[128,1024]{1,0:T(8,128)S(1)}, u32[]{:S(2)}) %copy-start.6) | copy-done | bytes 524312
  43.7 1.0 %collective-permute-start.1 = (bf16[16,64,256]{2,1,0:T(8,128)(2,1)S(1)}, bf16[16,64,256]{2,1,0:T(8,128)(2,1)S(1)}, u32[]{:S(2)}, u32[]{:S(2)}) collective-permute-start(bf16[16,64,256]{2,1,0:T(8,128)(2,1)S(1)} %get-tuple-element.41), channel_id=1, source_target_pairs={{0,128},{128,0},{1,129},{129,1},{2,130},{130,2},{3,131},{131,3},{4... | collective-permute-start | bytes 1572872 | tf_op jit(solution)/shard_map/ppermute | solution.py:319
  44.7 0.0 copy-start.7
  44.7 4.8 %all-to-all-start.3 = ((bf16[16,64,256]{2,1,0:T(8,128)(2,1)}), bf16[16,64,256]{2,1,0:T(8,128)(2,1)S(1)}, u32[]{:S(2)}, u32[]{:S(2)}) async-start(bf16[16,64,256]{2,1,0:T(8,128)(2,1)} %get-tuple-element.43), calls=%async_computation.3 | async-start | bytes 1048576 | tf_op jit(solution)/shard_map/all_to_all | solution.py:314
  49.6 0.0 copy-done.7
  49.6 4.6 %own_backward.1 = (bf16[64,1024]{1,0:T(8,128)(2,1)}, bf16[64,1024]{1,0:T(8,128)(2,1)}, f32[16,64,256]{2,1,0:T(8,128)S(1)}) custom-call(s32[4]{0:T(128)S(1)} %pad_add_fusion.refs_0_.place, bf16[1024,256]{1,0:T(8,128)(2,1)S(1)} %get-tuple-element.30.both_s, bf16[16,64,256]{2,1,0:T(8,128)(2,1)S(1)} %all-to-all-done.kv, ...), custom_call_target="tpu_custom_call" | custom-call | flops 1610612736 | tf_op jit(solution)/shard_map/own_backward/pallas_call | solution.py:282
  54.2 0.6 collective-permute-done.1
  54.8 1.0 %add_convert_fusion = bf16[16,64,256]{2,1,0:T(8,128)(2,1)} fusion(f32[16,64,256]{2,1,0:T(8,128)S(1)} %get-tuple-element.40, bf16[16,64,256]{2,1,0:T(8,128)(2,1)S(1)} %collective-permute-done.1), kind=kLoop, calls=%fused_computation | loop fusion | flops 786432 | bytes 2097152 | tf_op jit(solution)/shard_map/convert_element_type | solution.py:404
  55.8 3.9 %all-to-all-done.3 = bf16[16,64,256]{2,1,0:T(8,128)(2,1)S(1)} async-done(((bf16[16,64,256]{2,1,0:T(8,128)(2,1)}), bf16[16,64,256]{2,1,0:T(8,128)(2,1)S(1)}, u32[]{:S(2)}, u32[]{:S(2)}) %all-to-all-start.3) | async-done | bytes 524320 | tf_op jit(solution)/shard_map/all_to_all | solution.py:314
  59.7 3.6 %all-to-all-start.2 = ((bf16[16,64,256]{2,1,0:T(8,128)(2,1)}), bf16[16,64,256]{2,1,0:T(8,128)(2,1)S(1)}, u32[]{:S(2)}, u32[]{:S(2)}) async-start(bf16[16,64,256]{2,1,0:T(8,128)(2,1)} %add_convert_fusion), calls=%async_computation.2 | async-start | bytes 1048576 | tf_op jit(solution)/shard_map/all_to_all | solution.py:314
  63.3 0.1 reduce_sum.25
  63.4 0.6 slice_bitcast_fusion
  64.0 9.4 %all-to-all-done.2 = bf16[16,64,256]{2,1,0:T(8,128)(2,1)S(1)} async-done(((bf16[16,64,256]{2,1,0:T(8,128)(2,1)}), bf16[16,64,256]{2,1,0:T(8,128)(2,1)S(1)}, u32[]{:S(2)}, u32[]{:S(2)}) %all-to-all-start.2) | async-done | bytes 524320 | tf_op jit(solution)/shard_map/all_to_all | solution.py:314
  73.3 0.1 reduce_sum.24
  73.4 0.6 fusion
Async XLA Ops:
  2.2 7.9 %copy-start.8 = (s32[2]{0:T(128)S(1)}, s32[2]{0:T(128)}, u32[]{:S(2)}) copy-start(s32[2]{0:T(128)} %param.19) | copy-start | bytes 28
  2.2 9.2 %copy-start = (bf16[64,1024]{1,0:T(8,128)(2,1)S(1)}, bf16[64,1024]{1,0:T(8,128)(2,1)}, u32[]{:S(2)}) copy-start(bf16[64,1024]{1,0:T(8,128)(2,1)} %refs_1_.1) | copy-start | bytes 393220
  2.2 9.2 %copy-start.1 = (bf16[1,64,1024]{2,1,0:T(8,128)(2,1)S(1)}, bf16[1,64,1024]{2,1,0:T(8,128)(2,1)}, u32[]{:S(2)}) copy-start(bf16[1,64,1024]{2,1,0:T(8,128)(2,1)} %param.13) | copy-start | bytes 393220
  2.2 9.2 %copy-start.2 = (bf16[64,1024]{1,0:T(8,128)(2,1)S(1)}, bf16[64,1024]{1,0:T(8,128)(2,1)}, u32[]{:S(2)}) copy-start(bf16[64,1024]{1,0:T(8,128)(2,1)} %refs_3_.1) | copy-start | bytes 393220
  2.3 9.2 %copy-start.3 = (bf16[1,64,1024]{2,1,0:T(8,128)(2,1)S(1)}, bf16[1,64,1024]{2,1,0:T(8,128)(2,1)}, u32[]{:S(2)}) copy-start(bf16[1,64,1024]{2,1,0:T(8,128)(2,1)} %param.17) | copy-start | bytes 393220
  2.3 18.7 %all-to-all-start = ((bf16[16,64,256]{2,1,0:T(8,128)(2,1)}), bf16[16,64,256]{2,1,0:T(8,128)(2,1)S(1)}, u32[]{:S(2)}, u32[]{:S(2)}) async-start(bf16[16,64,256]{2,1,0:T(8,128)(2,1)} %copies.1), calls=%async_computation | async-start | bytes 1048576 | tf_op jit(solution)/shard_map/all_to_all | solution.py:314
  9.5 2.0 %copy-start.4 = (bf16[1,64,128]{2,1,0:T(8,128)(2,1)S(1)}, bf16[1,64,128]{2,1,0:T(8,128)(2,1)}, u32[]{:S(2)}) copy-start(bf16[1,64,128]{2,1,0:T(8,128)(2,1)} %param.14) | copy-start | bytes 49156
  9.5 2.0 %copy-start.5 = (bf16[1,64,128]{2,1,0:T(8,128)(2,1)S(1)}, bf16[1,64,128]{2,1,0:T(8,128)(2,1)}, u32[]{:S(2)}) copy-start(bf16[1,64,128]{2,1,0:T(8,128)(2,1)} %param.15) | copy-start | bytes 49156
  20.9 14.6 %collective-permute-start = (bf16[16,64,256]{2,1,0:T(8,128)(2,1)S(1)}, bf16[16,64,256]{2,1,0:T(8,128)(2,1)S(1)}, u32[]{:S(2)}, u32[]{:S(2)}) collective-permute-start(bf16[16,64,256]{2,1,0:T(8,128)(2,1)S(1)} %all-to-all-done.kv), channel_id=1, source_target_pairs={{0,128},{128,0},{1,129},{129,1},{2,130},{130,2},{3,131},{131,3},{4... | collective-permute-start | bytes 1572872 | tf_op jit(solution)/shard_map/ppermute | solution.py:319
  21.9 13.6 %all-to-all-start.1 = ((bf16[16,64,256]{2,1,0:T(8,128)(2,1)}), bf16[16,64,256]{2,1,0:T(8,128)(2,1)S(1)}, u32[]{:S(2)}, u32[]{:S(2)}) async-start(bf16[16,64,256]{2,1,0:T(8,128)(2,1)} %get-tuple-element.32), calls=%async_computation.1 | async-start | bytes 1048576 | tf_op jit(solution)/shard_map/all_to_all | solution.py:314
  42.9 0.8 %copy-start.6 = (f32[128,1024]{1,0:T(8,128)}, f32[128,1024]{1,0:T(8,128)S(1)}, u32[]{:S(2)}) copy-start(f32[128,1024]{1,0:T(8,128)S(1)} %get-tuple-element.38.dq_in) | copy-start | bytes 1572868
  43.7 11.1 %collective-permute-start.1 = (bf16[16,64,256]{2,1,0:T(8,128)(2,1)S(1)}, bf16[16,64,256]{2,1,0:T(8,128)(2,1)S(1)}, u32[]{:S(2)}, u32[]{:S(2)}) collective-permute-start(bf16[16,64,256]{2,1,0:T(8,128)(2,1)S(1)} %get-tuple-element.41), channel_id=1, source_target_pairs={{0,128},{128,0},{1,129},{129,1},{2,130},{130,2},{3,131},{131,3},{4... | collective-permute-start | bytes 1572872 | tf_op jit(solution)/shard_map/ppermute | solution.py:319
  44.7 4.9 %copy-start.7 = (f32[128,1024]{1,0:T(8,128)S(1)}, f32[128,1024]{1,0:T(8,128)}, u32[]{:S(2)}) copy-start(f32[128,1024]{1,0:T(8,128)} %copy-done.6) | copy-start | bytes 1572868
  44.7 15.0 %all-to-all-start.3 = ((bf16[16,64,256]{2,1,0:T(8,128)(2,1)}), bf16[16,64,256]{2,1,0:T(8,128)(2,1)S(1)}, u32[]{:S(2)}, u32[]{:S(2)}) async-start(bf16[16,64,256]{2,1,0:T(8,128)(2,1)} %get-tuple-element.43), calls=%async_computation.3 | async-start | bytes 1048576 | tf_op jit(solution)/shard_map/all_to_all | solution.py:314
  59.7 13.6 %all-to-all-start.2 = ((bf16[16,64,256]{2,1,0:T(8,128)(2,1)}), bf16[16,64,256]{2,1,0:T(8,128)(2,1)S(1)}, u32[]{:S(2)}, u32[]{:S(2)}) async-start(bf16[16,64,256]{2,1,0:T(8,128)(2,1)} %add_convert_fusion), calls=%async_computation.2 | async-start | bytes 1048576 | tf_op jit(solution)/shard_map/all_to_all | solution.py:314

commit v5 on v4

--- a/solution.py
+++ b/solution.py
@@ -25,8 +25,8 @@
     return lax.dot_general(a, b, (((ca,), (cb,)), ((), ())), preferred_element_type=F32)
 
 
-def at(chunk):
-    return pl.ds(pl.multiple_of(chunk * CHUNK, CHUNK), CHUNK)
+def at(chunk, size):
+    return pl.ds(pl.multiple_of(chunk * size, size), size)
 
 
 def chunks_of(count):
@@ -46,10 +46,6 @@
         self.own_len = jnp.clip(prompt_len - pair * half, 1, half)
         self.other_len = jnp.clip(prompt_len - (1 - pair) * half, 1, half)
         self.own_chunks = chunks_of(self.own_len)
-        self.other_chunks = chunks_of(self.other_len)
-        self.answer_chunks = jnp.where(
-            self.first < self.answer_len, chunks_of(self.first + rows), 0
-        )
         lane = lax.broadcasted_iota(jnp.int32, (1, rows * GROUP), 1)
         causal = self.first + lax.rem(lane, rows)
         flat = jnp.zeros_like(causal)
@@ -66,18 +62,12 @@
     answer_q,
     prompt_do,
     answer_do,
-    answer_k,
-    answer_v,
     q_t,
     both_s,
-    answer_copies,
     *,
     half,
 ):
     rows = prompt_q.shape[0]
-    for i in range(answer_copies.shape[0]):
-        answer_copies[i, :, KEYS] = answer_k[...]
-        answer_copies[i, :, VALUES] = answer_v[...]
     lanes = rows * GROUP
     where = Place(place, rows, half)
     for k, (q_ref, do_ref, first, length) in enumerate(
@@ -101,52 +91,50 @@
         q_t[:, side] = q_rows.T
 
 
-def block_of(kv, c, part, cols):
-    rows = part.stop - part.start
-    count = CHUNK // rows
-    return kv[pl.ds(c * count, count), part, cols].reshape(CHUNK, HEAD_SIZE)
+def block_of(kv, c, cols, size):
+    count = size // kv.shape[1]
+    return kv[at(c, count), :, cols].reshape(size, HEAD_SIZE)
 
 
 def put_block(dkv, c, dk, dv):
-    rows = dkv.shape[1]
-    count = CHUNK // rows
+    size, rows = dk.shape[0], dkv.shape[1]
+    count = size // rows
     for cols, d in ((KEYS, dk), (VALUES, dv)):
-        dkv[pl.ds(c * count, count), :, cols] = d.astype(dkv.dtype).reshape(count, rows, HEAD_SIZE)
-
-
-def masked_scores(kv, c, part, q_t, limit):
-    s = dot(block_of(kv, c, part, KEYS), q_t, 1, 0)
+        dkv[at(c, count), :, cols] = d.astype(dkv.dtype).reshape(count, rows, HEAD_SIZE)
+
+
+def masked_scores(kv, c, q_t, limit, size):
+    s = dot(block_of(kv, c, KEYS, size), q_t, 1, 0)
     key = lax.broadcasted_iota(jnp.int32, s.shape, 0)
-    return jnp.where(key <= limit - c * CHUNK, s, NEGATIVE)
-
-
-def score_pass(kv, part, q_t, side, limit, chunks, scores):
+    return jnp.where(key <= limit - c * size, s, NEGATIVE)
+
+
+def score_pass(kv, q_t, side, limit, chunks, size, scores):
     def step(c, run):
-        s = masked_scores(kv, c, part, q_t[:, side], limit)
-        scores[at(c), :] = s
-        for k in range(CHUNK // 8):
+        s = masked_scores(kv, c, q_t[:, side], limit, size)
+        scores[at(c, size), :] = s
+        for k in range(size // 8):
             run = jnp.maximum(run, s[k * 8 : (k + 1) * 8])
         return run
 
-    start = jnp.full((8, side.stop - side.start), NEGATIVE, F32)
-    return lax.fori_loop(0, chunks, step, start)
-
-
-def value_pass(kv, part, side, row_max, chunks, scores, o_t):
+    return lax.fori_loop(0, chunks, step, jnp.full((8, side.stop - side.start), NEGATIVE, F32))
+
+
+def value_pass(kv, side, row_max, chunks, size, scores, o_t):
     def step(c, sums):
-        p = jnp.exp2(scores[at(c), :] * TO_LOG2 - row_max)
-        for k in range(CHUNK // 8):
+        p = jnp.exp2(scores[at(c, size), :] * TO_LOG2 - row_max)
+        for k in range(size // 8):
             sums = sums + p[k * 8 : (k + 1) * 8]
-        scores[at(c), :] = p
-        o_t[:, side] += dot(block_of(kv, c, part, VALUES), p.astype(BF16), 0, 0)
+        scores[at(c, size), :] = p
+        o_t[:, side] += dot(block_of(kv, c, VALUES, size), p.astype(BF16), 0, 0)
         return sums
 
-    start = jnp.zeros((8, side.stop - side.start), F32)
-    return jnp.sum(lax.fori_loop(0, chunks, step, start), axis=0, keepdims=True)
-
-
-def gradients(kv, c, part, shares, side, do_t, both_s, delta, dkv, dq_t):
-    dp = dot(block_of(kv, c, part, VALUES), do_t[:, side], 1, 0)
+    sums = lax.fori_loop(0, chunks, step, jnp.zeros((8, side.stop - side.start), F32))
+    return jnp.sum(sums, axis=0, keepdims=True)
+
+
+def gradients(kv, c, size, shares, side, do_t, both_s, delta, dkv, dq_t):
+    dp = dot(block_of(kv, c, VALUES, size), do_t[:, side], 1, 0)
     ds = (shares * (dp - delta)).astype(BF16)
     put_block(
         dkv,
@@ -154,7 +142,7 @@
         dot(ds, both_s[side, KEYS], 1, 0) * SCALING,
         dot(shares.astype(BF16), both_s[side, VALUES], 1, 0),
     )
-    dq_t[:, side] += dot(block_of(kv, c, part, KEYS), ds, 0, 0)
+    dq_t[:, side] += dot(block_of(kv, c, KEYS, size), ds, 0, 0)
 
 
 def blank(dkv, begin):
@@ -185,12 +173,11 @@
     rows = kv.shape[1]
     every = sides(q_t)[2]
     where = Place(place, rows, kv.shape[0] * rows)
-    part = slice(0, rows)
-    run = score_pass(kv, part, q_t, every, where.own_limit, where.own_chunks, scores)
+    run = score_pass(kv, q_t, every, where.own_limit, where.own_chunks, CHUNK, scores)
     row_max = jnp.max(run, axis=0, keepdims=True) * TO_LOG2
     o_t[...] = jnp.zeros_like(o_t)
     stats[0:1, :] = row_max
-    stats[1:2, :] = value_pass(kv, part, every, row_max, where.own_chunks, scores, o_t)
+    stats[1:2, :] = value_pass(kv, every, row_max, where.own_chunks, CHUNK, scores, o_t)
 
 
 def other_kernel(
@@ -215,21 +202,19 @@
     rows = kv.shape[1]
     prompt, answer, every = sides(q_t)
     where = Place(place, rows, kv.shape[0] * rows)
-    part = slice(0, rows)
-    chunks = where.other_chunks
-    run = score_pass(kv, part, q_t, every, where.other_limit, chunks, scores)
-    answer_run = score_pass(
-        answer_kv, part, q_t, answer, where.answer_limit, where.answer_chunks, answer_scores
-    )
+    size = kv.shape[0] * rows
+    pieces = jnp.minimum(where.prompt_len, 1)
+    run = score_pass(kv, q_t, every, where.other_limit, pieces, size, scores)
+    answer_run = score_pass(answer_kv, q_t, answer, where.answer_limit, pieces, size, answer_scores)
     run = jnp.concatenate([run[:, prompt], jnp.maximum(run[:, answer], answer_run)], axis=1)
     do_t[...] = both_s[:, VALUES].T
     own_max = stats[0:1, :]
     row_max = jnp.maximum(jnp.max(run, axis=0, keepdims=True) * TO_LOG2, own_max)
     shrink = jnp.exp2(own_max - row_max)
     o_t[...] = o_in[...] * shrink
-    total = value_pass(kv, part, every, row_max, chunks, scores, o_t) + stats[1:2, :] * shrink
+    total = value_pass(kv, every, row_max, pieces, size, scores, o_t) + stats[1:2, :] * shrink
     answer_total = value_pass(
-        answer_kv, part, answer, row_max[:, answer], where.answer_chunks, answer_scores, o_t
+        answer_kv, answer, row_max[:, answer], pieces, size, answer_scores, o_t
     )
     total = jnp.concatenate([total[:, prompt], total[:, answer] + answer_total], axis=1)
     inverse = 1.0 / total
@@ -241,17 +226,17 @@
     write_rows(answer_out, out_t[:, answer], rows, where.first, where.answer_len)
     dq_t[...] = jnp.zeros_like(dq_t)
 
-    def run(kv, scores, side, chunks, dkv):
-        def step(c, _):
-            shares = scores[at(c), :] * inverse[:, side]
-            gradients(kv, c, part, shares, side, do_t, both_s, delta[:, side], dkv, dq_t)
+    for kv, scores, side, dkv in (
+        (kv, scores, every, dkv),
+        (answer_kv, answer_scores, answer, answer_dkv),
+    ):
+
+        def step(c, _, kv=kv, scores=scores, side=side, dkv=dkv):
+            shares = scores[at(c, size), :] * inverse[:, side]
+            gradients(kv, c, size, shares, side, do_t, both_s, delta[:, side], dkv, dq_t)
             return 0
 
-        lax.fori_loop(0, chunks, step, 0)
-        blank(dkv, chunks)
-
-    run(kv, scores, every, chunks, dkv)
-    run(answer_kv, answer_scores, answer, where.answer_chunks, answer_dkv)
+        lax.fori_loop(0, pieces, step, 0)
 
 
 def own_backward_kernel(
@@ -260,16 +245,15 @@
     rows = kv.shape[1]
     prompt, answer, every = sides(q_t)
     where = Place(place, rows, kv.shape[0] * rows)
-    part = slice(0, rows)
     do_t[...] = both_s[:, VALUES].T
     q_t[...] = both_s[:, KEYS].T
     dq_t[...] = dq_in[...]
     log_total, delta = factors[0:1, :], factors[1:2, :]
 
     def step(c, _):
-        s = masked_scores(kv, c, part, q_t[...], where.own_limit)
+        s = masked_scores(kv, c, q_t[...], where.own_limit, CHUNK)
         shares = jnp.exp2(s * TO_LOG2 - log_total)
-        gradients(kv, c, part, shares, every, do_t, both_s, delta, dkv, dq_t)
+        gradients(kv, c, CHUNK, shares, every, do_t, both_s, delta, dkv, dq_t)
         return 0
 
     lax.fori_loop(0, where.own_chunks, step, 0)
@@ -291,23 +275,46 @@
     )(*arrays)
 
 
-def copies_of(keys, values, count):
-    rows = keys.shape[0]
-
-    def kernel(k, v, out):
-        for i in range(count):
-            out[i, :, KEYS] = k[...]
-            out[i, :, VALUES] = v[...]
+def copies_of(parts, count):
+    shape = jax.ShapeDtypeStruct((count, parts[0].shape[0], 2 * HEAD_SIZE), BF16)
+
+    def kernel(pk, pv, ak, av, prompt, answer):
+        for k, v, out in ((pk, pv, prompt), (ak, av, answer)):
+            for i in range(count):
+                out[i, :, KEYS] = k[...]
+                out[i, :, VALUES] = v[...]
 
     return pl.pallas_call(
         kernel,
-        out_shape=jax.ShapeDtypeStruct((count, rows, 2 * HEAD_SIZE), BF16),
-        in_specs=[VMEM] * 2,
-        out_specs=VMEM,
+        out_shape=[shape] * 2,
+        in_specs=[VMEM] * 4,
+        out_specs=[VMEM] * 2,
         compiler_params=pltpu.CompilerParams(vmem_limit_bytes=67043328),
         cost_estimate=pl.CostEstimate(flops=10**6, bytes_accessed=0, transcendentals=0),
         name="copies",
-    )(keys, values)
+    )(*parts)
+
+
+def collected(prompt_parts, answer_parts):
+    shape = jax.ShapeDtypeStruct((prompt_parts.shape[1], HEAD_SIZE), BF16)
+
+    def kernel(prompt_parts, answer_parts, prompt_k, prompt_v, answer_k, answer_v):
+        for parts, k, v in (
+            (prompt_parts, prompt_k, prompt_v),
+            (answer_parts, answer_k, answer_v),
+        ):
+            total = jnp.sum(parts[...].astype(F32), axis=0).astype(BF16)
+            k[...] = total[:, KEYS]
+            v[...] = total[:, VALUES]
+
+    return pl.pallas_call(
+        kernel,
+        out_shape=[shape] * 4,
+        in_specs=[VMEM] * 2,
+        out_specs=[VMEM] * 4,
+        compiler_params=pltpu.CompilerParams(vmem_limit_bytes=16 * 1024 * 1024),
+        name="collected",
+    )(prompt_parts, answer_parts)
 
 
 def exchanged(pieces):
@@ -336,7 +343,14 @@
     pair_index = lax.axis_index("pair")
     count = lax.axis_size("ctx")
     half = count * rows
-    own_kv = exchanged(copies_of(prompt_key_rows, prompt_value_rows, count))
+    prompt_copies, answer_copies = copies_of(
+        (prompt_key_rows, prompt_value_rows, response_key_rows[0], response_value_rows[0]), count
+    )
+    own_kv, answer_copies, prompt_length, answer_lengths = lax.optimization_barrier(
+        (exchanged(prompt_copies), answer_copies, prompt_length, answer_lengths)
+    )
+    other_kv = to_partner(own_kv)
+    answer_kv = exchanged(answer_copies)
     place = jnp.stack(
         [
             pair_index,
@@ -349,28 +363,15 @@
     out = ((rows, GROUP * HEAD_SIZE), BF16)
     stat = ((8, 2 * lanes), F32)
     kv_shape = (count, rows, 2 * HEAD_SIZE)
-    q_t, both_s, answer_copies = call(
+    q_t, both_s = call(
         lambda *refs: prepare_kernel(*refs, half=half),
         "prepare",
-        (
-            place,
-            prompt_queries,
-            answer_queries[0],
-            prompt_cotangent,
-            answer_cotangent[0],
-            response_key_rows[0],
-            response_value_rows[0],
-        ),
-        [(wide, BF16), (tall, BF16), (kv_shape, BF16)],
+        (place, prompt_queries, answer_queries[0], prompt_cotangent, answer_cotangent[0]),
+        [(wide, BF16), (tall, BF16)],
         [],
         10**9,
         8,
     )
-    own_kv, answer_copies, q_t, both_s = lax.optimization_barrier(
-        (own_kv, answer_copies, q_t, both_s)
-    )
-    other_kv = to_partner(own_kv)
-    answer_kv = exchanged(answer_copies)
     flops = 2 * half * lanes * HEAD_SIZE
     o_t, stats = call(
         own_forward_kernel,
@@ -391,7 +392,7 @@
         16,
     )
     from_partner = to_partner(other_dkv)
-    answer_grad = exchanged(answer_dkv).astype(F32).sum(axis=0).astype(BF16)
+    answer_parts = exchanged(answer_dkv)
     prompt_dq, answer_dq, own_dkv = call(
         own_backward_kernel,
         "own_backward",
@@ -402,16 +403,17 @@
         16,
     )
     prompt_dkv = (own_dkv + from_partner.astype(F32)).astype(BF16)
-    prompt_grad = exchanged(prompt_dkv).astype(F32).sum(axis=0).astype(BF16)
+    prompt_parts = exchanged(prompt_dkv)
+    prompt_k, prompt_v, answer_k, answer_v = collected(prompt_parts, answer_parts)
     return (
         prompt_out,
         answer_out[None],
         prompt_dq,
-        prompt_grad[:, KEYS],
-        prompt_grad[:, VALUES],
+        prompt_k,
+        prompt_v,
         answer_dq[None],
-        answer_grad[None, :, KEYS],
-        answer_grad[None, :, VALUES],
+        answer_k[None],
+        answer_v[None],
     )
 
 

time: 74.3 us -> 73.9 us (level)
  blocking collectives: 0 us -> 31.9 us
  waiting for transfers between devices: 29.3 us -> 11.9 us
  starting transfers between devices: 21.2 us -> 9.39 us
  Pallas kernels: 17.6 us -> 15.6 us
  other arithmetic: 1.84 us -> 0.87 us
    all_to_all x0 -> x2, blocking collectives: none -> 31.9 us  [exchanged(): lax.all_to_all(pieces, 'ctx', split_axis=0, concat_axis=0, tiled=True)]
    all_to_all x4 -> x2, waiting for transfers between devices: 28.7 us -> 8.67 us  [exchanged(): lax.all_to_all(pieces, 'ctx', split_axis=0, concat_axis=0, tiled=True)]
    all_to_all x4 -> x2, starting transfers between devices: 19.2 us -> 7.27 us  [exchanged(): lax.all_to_all(pieces, 'ctx', split_axis=0, concat_axis=0, tiled=True)]
    pallas_call x4, Pallas kernels: 16 us -> 13 us  [call(): pl.pallas_call(kernel, out_shape=[jax.ShapeDtypeStruct(*o) for o in outs]...]
    ppermute x2, waiting for transfers between devices: 0.57 us -> 3.22 us  [to_partner(): lax.ppermute(block, 'pair', [(i, count - 1 - i) for i in range(count)])]
    pallas_call x1 -> x2, Pallas kernels: 1.6 us -> 2.58 us  [the longest x1 1.82 us: copies_of(): pl.pallas_call(kernel, out_shape=[shape] * 2, in_specs=[VMEM] * 4, out_sp...]
    convert_element_type x1, other arithmetic: 0.97 us -> 0.15 us  [body(): prompt_dkv = (own_dkv + from_partner.astype(F32)).astype(BF16)]
  transfers between devices with their start and end apart: 6 -> 4, of which waited for: 5 -> 3; matrix products, arithmetic and copies ran while one was open for 4% -> 2% of each run, Pallas kernels for 12% -> 7%
where the time goes in v5:
time: 73.9 us; the launch traced here: 73 us
  blocking collectives  31.9 us (43%)
  Pallas kernels  15.6 us (21%)
  waiting for transfers between devices  11.9 us (16%)
  starting transfers between devices  9.39 us (13%)
  local copies, waits for them, and re-layouts  2.05 us (3%)
  between operations  1.37 us (2%)
  other arithmetic  0.87 us (1%)
    all_to_all x2, blocking collectives, exchanged(): lax.all_to_all(pieces, 'ctx', split_axis=0, concat_axis=0, tiled=True)  31.9 us
    pallas_call x4, Pallas kernels, call(): pl.pallas_call(kernel, out_shape=[jax.ShapeDtypeStruct(*o) for o in outs]...  13 us
    all_to_all x2, waiting for transfers between devices, exchanged(): lax.all_to_all(pieces, 'ctx', split_axis=0, concat_axis=0, tiled=True)  8.67 us
    all_to_all x2, starting transfers between devices, exchanged(): lax.all_to_all(pieces, 'ctx', split_axis=0, concat_axis=0, tiled=True)  7.27 us
    ppermute x2, waiting for transfers between devices, to_partner(): lax.ppermute(block, 'pair', [(i, count - 1 - i) for i in range(count)])  3.22 us
    ppermute x2, starting transfers between devices, to_partner(): lax.ppermute(block, 'pair', [(i, count - 1 - i) for i in range(count)])  2.12 us
    pallas_call x1, Pallas kernels, copies_of(): pl.pallas_call(kernel, out_shape=[shape] * 2, in_specs=[VMEM] * 4, out_sp...  1.82 us
  transfers between devices with their start and end apart: 4, of which 3 were waited for; matrix products, arithmetic and copies ran while one was open for 2% of the time, Pallas kernels for 7%

profile of v5, /device:TPU:160, one launch (start us, length us, event | category | flops | bytes accessed | tf_op | source)
XLA Modules:
  0.0 73.0 jit_solution(9861399466371689842)
XLA Ops:
  0.6 1.8 %copies.1 = (bf16[16,64,256]{2,1,0:T(8,128)(2,1)}, bf16[16,64,256]{2,1,0:T(8,128)(2,1)}) custom-call(bf16[64,128]{1,0:T(8,128)(2,1)} %pk.1, bf16[64,128]{1,0:T(8,128)(2,1)} %pv.1, bf16[64,128]{1,0:T(8,128)(2,1)} %bitcast.12, bf16[64,128]{1,0:T(8,128)(2,1)} %bitcast.13), custom_call_target="tpu_custom_call" | custom-call | flops 1000000 | tf_op jit(solution)/shard_map/copies/pallas_call | solution.py:287
  2.5 18.5 %all_to_all.20.kv = bf16[16,64,256]{2,1,0:T(8,128)(2,1)S(1)} all-to-all(bf16[16,64,256]{2,1,0:T(8,128)(2,1)} %get-tuple-element.31), channel_id=1, replica_groups=mesh['pair'=2,'ctx'=16,'head'=8] {'ctx'}, dimensions={0} | all-to-all | bytes 1048576 | tf_op jit(solution)/shard_map/all_to_all | solution.py:321
  21.0 0.0 copy-start
  21.0 0.0 copy-start.1
  21.0 0.0 copy-start.2
  21.0 0.0 copy-start.3
  21.0 1.1 %collective-permute-start = (bf16[16,64,256]{2,1,0:T(8,128)(2,1)S(1)}, bf16[16,64,256]{2,1,0:T(8,128)(2,1)S(1)}, u32[]{:S(2)}, u32[]{:S(2)}) collective-permute-start(bf16[16,64,256]{2,1,0:T(8,128)(2,1)S(1)} %all_to_all.20.kv), channel_id=1, source_target_pairs={{0,128},{128,0},{1,129},{129,1},{2,130},{130,2},{3,131},{131,3},{4... | collective-permute-start | bytes 1572872 | tf_op jit(solution)/shard_map/ppermute | solution.py:326
  22.1 3.6 %all-to-all-start.1 = ((bf16[16,64,256]{2,1,0:T(8,128)(2,1)}), bf16[16,64,256]{2,1,0:T(8,128)(2,1)S(1)}, u32[]{:S(2)}, u32[]{:S(2)}) async-start(bf16[16,64,256]{2,1,0:T(8,128)(2,1)} %get-tuple-element.38), calls=%async_computation.1 | async-start | bytes 1048576 | tf_op jit(solution)/shard_map/all_to_all | solution.py:321
  26.3 0.0 copy-start.6
  26.3 0.6 copy-done.6
  27.0 0.6 dynamic_slice.4
  27.6 0.7 pad_add_fusion.refs_0_.place
  28.3 0.0 copy-done
  28.3 0.0 copy-done.1
  28.3 0.0 copy-done.2
  28.3 0.0 copy-done.3
  28.3 0.7 prepare.1
  29.0 1.6 %own_forward.1 = (f32[128,1024]{1,0:T(8,128)S(1)}, f32[8,1024]{1,0:T(8,128)S(1)}) custom-call(s32[4]{0:T(128)S(1)} %pad_add_fusion.refs_0_.place, bf16[128,1024]{1,0:T(8,128)(2,1)S(1)} %get-tuple-element.35.q_t, bf16[16,64,256]{2,1,0:T(8,128)(2,1)S(1)} %all_to_all.20.kv), custom_call_target="tpu_custom_call" | custom-call | flops 1073741824 | tf_op jit(solution)/shard_map/own_forward/pallas_call | solution.py:266
  30.6 5.1 %all-to-all-done.1.answer_kv = bf16[16,64,256]{2,1,0:T(8,128)(2,1)S(1)} async-done(((bf16[16,64,256]{2,1,0:T(8,128)(2,1)}), bf16[16,64,256]{2,1,0:T(8,128)(2,1)S(1)}, u32[]{:S(2)}, u32[]{:S(2)}) %all-to-all-start.1) | async-done | bytes 524320 | tf_op jit(solution)/shard_map/all_to_all | solution.py:321
  35.7 0.0 collective-permute-done.kv
  35.7 7.6 %other.1 = (bf16[64,1024]{1,0:T(8,128)(2,1)}, bf16[64,1024]{1,0:T(8,128)(2,1)}, bf16[16,64,256]{2,1,0:T(8,128)(2,1)S(1)}, bf16[16,64,256]{2,1,0:T(8,128)(2,1)}, ...) custom-call(s32[4]{0:T(128)S(1)} %pad_add_fusion.refs_0_.place, bf16[128,1024]{1,0:T(8,128)(2,1)S(1)} %get-tuple-element.35.q_t, ...), custom_call_target="tpu_custom_call" | custom-call | flops 2147483648 | tf_op jit(solution)/shard_map/other/pallas_call | solution.py:266
  43.4 0.0 copy-start.4
  43.4 0.8 %copy-done.4 = f32[128,1024]{1,0:T(8,128)} copy-done((f32[128,1024]{1,0:T(8,128)}, f32[128,1024]{1,0:T(8,128)S(1)}, u32[]{:S(2)}) %copy-start.4) | copy-done | bytes 524312
  44.2 1.0 %collective-permute-start.1 = (bf16[16,64,256]{2,1,0:T(8,128)(2,1)S(1)}, bf16[16,64,256]{2,1,0:T(8,128)(2,1)S(1)}, u32[]{:S(2)}, u32[]{:S(2)}) collective-permute-start(bf16[16,64,256]{2,1,0:T(8,128)(2,1)S(1)} %get-tuple-element.47), channel_id=1, source_target_pairs={{0,128},{128,0},{1,129},{129,1},{2,130},{130,2},{3,131},{131,3},{4... | collective-permute-start | bytes 1572872 | tf_op jit(solution)/shard_map/ppermute | solution.py:326
  45.2 0.0 copy-start.5
  45.2 3.7 %all-to-all-start.3 = ((bf16[16,64,256]{2,1,0:T(8,128)(2,1)}), bf16[16,64,256]{2,1,0:T(8,128)(2,1)S(1)}, u32[]{:S(2)}, u32[]{:S(2)}) async-start(bf16[16,64,256]{2,1,0:T(8,128)(2,1)} %get-tuple-element.48), calls=%async_computation.3 | async-start | bytes 1048576 | tf_op jit(solution)/shard_map/all_to_all | solution.py:321
  48.9 0.0 copy-done.5
  48.9 3.1 %own_backward.1 = (bf16[64,1024]{1,0:T(8,128)(2,1)}, bf16[64,1024]{1,0:T(8,128)(2,1)}, f32[16,64,256]{2,1,0:T(8,128)S(1)}) custom-call(s32[4]{0:T(128)S(1)} %pad_add_fusion.refs_0_.place, bf16[1024,256]{1,0:T(8,128)(2,1)S(1)} %get-tuple-element.36.both_s, bf16[16,64,256]{2,1,0:T(8,128)(2,1)S(1)} %all_to_all.20.kv, f32[8,1024]{1,0:T(8,128)S(1)} %get-tuple-element.43.factors, ...), custom_call_target="tpu_custom_call" | custom-call | flops 1610612736 | tf_op jit(solution)/shard_map/own_backward/pallas_call | solution.py:266
  52.0 3.2 %collective-permute-done.1 = bf16[16,64,256]{2,1,0:T(8,128)(2,1)S(1)} collective-permute-done((bf16[16,64,256]{2,1,0:T(8,128)(2,1)S(1)}, bf16[16,64,256]{2,1,0:T(8,128)(2,1)S(1)}, u32[]{:S(2)}, u32[]{:S(2)}) %collective-permute-start.1) | collective-permute-done | bytes 524320 | tf_op jit(solution)/shard_map/ppermute | solution.py:326
  55.2 0.2 add_convert_fusion
  55.4 3.6 %all-to-all-done.3.answer_parts = bf16[16,64,256]{2,1,0:T(8,128)(2,1)S(1)} async-done(((bf16[16,64,256]{2,1,0:T(8,128)(2,1)}), bf16[16,64,256]{2,1,0:T(8,128)(2,1)S(1)}, u32[]{:S(2)}, u32[]{:S(2)}) %all-to-all-start.3) | async-done | bytes 524320 | tf_op jit(solution)/shard_map/all_to_all | solution.py:321
  58.9 13.3 %all_to_all.21.prompt_parts = bf16[16,64,256]{2,1,0:T(8,128)(2,1)S(1)} all-to-all(bf16[16,64,256]{2,1,0:T(8,128)(2,1)S(1)} %add_convert_fusion), channel_id=1, replica_groups=mesh['pair'=2,'ctx'=16,'head'=8] {'ctx'}, dimensions={0} | all-to-all | bytes 1048576 | tf_op jit(solution)/shard_map/all_to_all | solution.py:321
  72.3 0.8 %collected.1 = (bf16[64,128]{1,0:T(8,128)(2,1)}, bf16[64,128]{1,0:T(8,128)(2,1)}, bf16[64,128]{1,0:T(8,128)(2,1)}, bf16[64,128]{1,0:T(8,128)(2,1)}) custom-call(bf16[16,64,256]{2,1,0:T(8,128)(2,1)S(1)} %all_to_all.21.prompt_parts, bf16[16,64,256]{2,1,0:T(8,128)(2,1)S(1)} %all-to-all-done.3.answer_parts), custom_call_target="tpu_custom_call" | custom-call | tf_op jit(solution)/shard_map/collected/pallas_call | solution.py:310
Async XLA Ops:
  21.0 7.3 %copy-start = (bf16[64,1024]{1,0:T(8,128)(2,1)S(1)}, bf16[64,1024]{1,0:T(8,128)(2,1)}, u32[]{:S(2)}) copy-start(bf16[64,1024]{1,0:T(8,128)(2,1)} %refs_1_.1) | copy-start | bytes 393220
  21.0 7.3 %copy-start.1 = (bf16[1,64,1024]{2,1,0:T(8,128)(2,1)S(1)}, bf16[1,64,1024]{2,1,0:T(8,128)(2,1)}, u32[]{:S(2)}) copy-start(bf16[1,64,1024]{2,1,0:T(8,128)(2,1)} %param.13) | copy-start | bytes 393220
  21.0 7.3 %copy-start.2 = (bf16[64,1024]{1,0:T(8,128)(2,1)S(1)}, bf16[64,1024]{1,0:T(8,128)(2,1)}, u32[]{:S(2)}) copy-start(bf16[64,1024]{1,0:T(8,128)(2,1)} %refs_3_.1) | copy-start | bytes 393220
  21.0 7.3 %copy-start.3 = (bf16[1,64,1024]{2,1,0:T(8,128)(2,1)S(1)}, bf16[1,64,1024]{2,1,0:T(8,128)(2,1)}, u32[]{:S(2)}) copy-start(bf16[1,64,1024]{2,1,0:T(8,128)(2,1)} %param.17) | copy-start | bytes 393220
  21.0 14.7 %collective-permute-start = (bf16[16,64,256]{2,1,0:T(8,128)(2,1)S(1)}, bf16[16,64,256]{2,1,0:T(8,128)(2,1)S(1)}, u32[]{:S(2)}, u32[]{:S(2)}) collective-permute-start(bf16[16,64,256]{2,1,0:T(8,128)(2,1)S(1)} %all_to_all.20.kv), channel_id=1, source_target_pairs={{0,128},{128,0},{1,129},{129,1},{2,130},{130,2},{3,131},{131,3},{4... | collective-permute-start | bytes 1572872 | tf_op jit(solution)/shard_map/ppermute | solution.py:326
  22.1 13.6 %all-to-all-start.1 = ((bf16[16,64,256]{2,1,0:T(8,128)(2,1)}), bf16[16,64,256]{2,1,0:T(8,128)(2,1)S(1)}, u32[]{:S(2)}, u32[]{:S(2)}) async-start(bf16[16,64,256]{2,1,0:T(8,128)(2,1)} %get-tuple-element.38), calls=%async_computation.1 | async-start | bytes 1048576 | tf_op jit(solution)/shard_map/all_to_all | solution.py:321
  26.3 0.7 copy-start.6
  43.4 0.8 %copy-start.4 = (f32[128,1024]{1,0:T(8,128)}, f32[128,1024]{1,0:T(8,128)S(1)}, u32[]{:S(2)}) copy-start(f32[128,1024]{1,0:T(8,128)S(1)} %get-tuple-element.44.dq_in) | copy-start | bytes 1572868
  44.2 11.1 %collective-permute-start.1 = (bf16[16,64,256]{2,1,0:T(8,128)(2,1)S(1)}, bf16[16,64,256]{2,1,0:T(8,128)(2,1)S(1)}, u32[]{:S(2)}, u32[]{:S(2)}) collective-permute-start(bf16[16,64,256]{2,1,0:T(8,128)(2,1)S(1)} %get-tuple-element.47), channel_id=1, source_target_pairs={{0,128},{128,0},{1,129},{129,1},{2,130},{130,2},{3,131},{131,3},{4... | collective-permute-start | bytes 1572872 | tf_op jit(solution)/shard_map/ppermute | solution.py:326
  45.2 3.7 %copy-start.5 = (f32[128,1024]{1,0:T(8,128)S(1)}, f32[128,1024]{1,0:T(8,128)}, u32[]{:S(2)}) copy-start(f32[128,1024]{1,0:T(8,128)} %copy-done.4) | copy-start | bytes 1572868
  45.2 13.8 %all-to-all-start.3 = ((bf16[16,64,256]{2,1,0:T(8,128)(2,1)}), bf16[16,64,256]{2,1,0:T(8,128)(2,1)S(1)}, u32[]{:S(2)}, u32[]{:S(2)}) async-start(bf16[16,64,256]{2,1,0:T(8,128)(2,1)} %get-tuple-element.48), calls=%async_computation.3 | async-start | bytes 1048576 | tf_op jit(solution)/shard_map/all_to_all | solution.py:321

commit v6 on v5

--- a/solution.py
+++ b/solution.py
@@ -62,12 +62,18 @@
     answer_q,
     prompt_do,
     answer_do,
+    answer_k,
+    answer_v,
     q_t,
     both_s,
+    answer_copies,
     *,
     half,
 ):
     rows = prompt_q.shape[0]
+    for i in range(answer_copies.shape[0]):
+        answer_copies[i, :, KEYS] = answer_k[...]
+        answer_copies[i, :, VALUES] = answer_v[...]
     lanes = rows * GROUP
     where = Place(place, rows, half)
     for k, (q_ref, do_ref, first, length) in enumerate(
@@ -262,37 +268,37 @@
     write_rows(answer_dq, dq_t[:, answer] * SCALING, rows)
 
 
-def call(kernel, name, arrays, outs, scratch, flops, mib):
+def call(kernel, name, arrays, outs, scratch, flops, mib, aliases=None):
     return pl.pallas_call(
         kernel,
         out_shape=[jax.ShapeDtypeStruct(*o) for o in outs],
         in_specs=[SMEM] + [VMEM] * (len(arrays) - 1),
         out_specs=[VMEM] * len(outs),
         scratch_shapes=[pltpu.VMEM(*s) for s in scratch],
+        input_output_aliases=aliases or {},
         compiler_params=pltpu.CompilerParams(vmem_limit_bytes=mib * 1024 * 1024),
         cost_estimate=pl.CostEstimate(flops=flops, bytes_accessed=0, transcendentals=0),
         name=name,
     )(*arrays)
 
 
-def copies_of(parts, count):
-    shape = jax.ShapeDtypeStruct((count, parts[0].shape[0], 2 * HEAD_SIZE), BF16)
-
-    def kernel(pk, pv, ak, av, prompt, answer):
-        for k, v, out in ((pk, pv, prompt), (ak, av, answer)):
-            for i in range(count):
-                out[i, :, KEYS] = k[...]
-                out[i, :, VALUES] = v[...]
+def copies_of(keys, values, count):
+    rows = keys.shape[0]
+
+    def kernel(k, v, out):
+        for i in range(count):
+            out[i, :, KEYS] = k[...]
+            out[i, :, VALUES] = v[...]
 
     return pl.pallas_call(
         kernel,
-        out_shape=[shape] * 2,
-        in_specs=[VMEM] * 4,
-        out_specs=[VMEM] * 2,
+        out_shape=jax.ShapeDtypeStruct((count, rows, 2 * HEAD_SIZE), BF16),
+        in_specs=[VMEM] * 2,
+        out_specs=VMEM,
         compiler_params=pltpu.CompilerParams(vmem_limit_bytes=67043328),
         cost_estimate=pl.CostEstimate(flops=10**6, bytes_accessed=0, transcendentals=0),
         name="copies",
-    )(*parts)
+    )(keys, values)
 
 
 def collected(prompt_parts, answer_parts):
@@ -343,14 +349,7 @@
     pair_index = lax.axis_index("pair")
     count = lax.axis_size("ctx")
     half = count * rows
-    prompt_copies, answer_copies = copies_of(
-        (prompt_key_rows, prompt_value_rows, response_key_rows[0], response_value_rows[0]), count
-    )
-    own_kv, answer_copies, prompt_length, answer_lengths = lax.optimization_barrier(
-        (exchanged(prompt_copies), answer_copies, prompt_length, answer_lengths)
-    )
-    other_kv = to_partner(own_kv)
-    answer_kv = exchanged(answer_copies)
+    own_kv = exchanged(copies_of(prompt_key_rows, prompt_value_rows, count))
     place = jnp.stack(
         [
             pair_index,
@@ -363,15 +362,28 @@
     out = ((rows, GROUP * HEAD_SIZE), BF16)
     stat = ((8, 2 * lanes), F32)
     kv_shape = (count, rows, 2 * HEAD_SIZE)
-    q_t, both_s = call(
+    q_t, both_s, answer_copies = call(
         lambda *refs: prepare_kernel(*refs, half=half),
         "prepare",
-        (place, prompt_queries, answer_queries[0], prompt_cotangent, answer_cotangent[0]),
-        [(wide, BF16), (tall, BF16)],
+        (
+            place,
+            prompt_queries,
+            answer_queries[0],
+            prompt_cotangent,
+            answer_cotangent[0],
+            response_key_rows[0],
+            response_value_rows[0],
+        ),
+        [(wide, BF16), (tall, BF16), (kv_shape, BF16)],
         [],
         10**9,
         8,
     )
+    own_kv, answer_copies, q_t, both_s = lax.optimization_barrier(
+        (own_kv, answer_copies, q_t, both_s)
+    )
+    other_kv = to_partner(own_kv)
+    answer_kv = exchanged(answer_copies)
     flops = 2 * half * lanes * HEAD_SIZE
     o_t, stats = call(
         own_forward_kernel,
@@ -390,6 +402,7 @@
         [((half, 2 * lanes), F32), ((half, lanes), F32), (wide, F32), (wide, BF16)],
         16 * flops,
         16,
+        aliases={5: 4},
     )
     from_partner = to_partner(other_dkv)
     answer_parts = exchanged(answer_dkv)

time: 73.9 us -> 72.7 us (0.984)
  blocking collectives: 31.9 us -> 13.3 us
  waiting for transfers between devices: 11.9 us -> 20.7 us
  starting transfers between devices: 9.39 us -> 16.3 us
  Pallas kernels: 15.6 us -> 18.7 us
  local copies, waits for them, and re-layouts: 2.05 us -> 0.62 us
    all_to_all x2 -> x1, blocking collectives: 31.9 us -> 13.3 us  [exchanged(): lax.all_to_all(pieces, 'ctx', split_axis=0, concat_axis=0, tiled=True)]
    all_to_all x2 -> x3, waiting for transfers between devices: 8.67 us -> 18.8 us  [exchanged(): lax.all_to_all(pieces, 'ctx', split_axis=0, concat_axis=0, tiled=True)]
    all_to_all x2 -> x3, starting transfers between devices: 7.27 us -> 14.3 us  [exchanged(): lax.all_to_all(pieces, 'ctx', split_axis=0, concat_axis=0, tiled=True)]
    pallas_call x4, Pallas kernels: 13 us -> 16.3 us  [call(): pl.pallas_call(kernel, out_shape=[jax.ShapeDtypeStruct(*o) for o in outs]...]
    unnamed x14, local copies, waits for them, and re-layouts: 1.47 us -> 0.03 us
    ppermute x2, waiting for transfers between devices: 3.22 us -> 1.86 us  [to_partner(): lax.ppermute(block, 'pair', [(i, count - 1 - i) for i in range(count)])]
  transfers between devices with their start and end apart: 4 -> 5, of which waited for: 3 -> 4; matrix products, arithmetic and copies ran while one was open for 2% -> 2% of each run, Pallas kernels for 7% -> 12%
where the time goes in v6:
time: 72.7 us; the launch traced here: 72 us
  waiting for transfers between devices  20.7 us (28%)
  Pallas kernels  18.7 us (26%)
  starting transfers between devices  16.3 us (22%)
  blocking collectives  13.3 us (18%)
  between operations  1.41 us (2%)
  other arithmetic  0.87 us (1%)
    all_to_all x3, waiting for transfers between devices, exchanged(): lax.all_to_all(pieces, 'ctx', split_axis=0, concat_axis=0, tiled=True)  18.8 us
    pallas_call x4, Pallas kernels, call(): pl.pallas_call(kernel, out_shape=[jax.ShapeDtypeStruct(*o) for o in outs]...  16.3 us
    all_to_all x3, starting transfers between devices, exchanged(): lax.all_to_all(pieces, 'ctx', split_axis=0, concat_axis=0, tiled=True)  14.3 us
    all_to_all x1, blocking collectives, exchanged(): lax.all_to_all(pieces, 'ctx', split_axis=0, concat_axis=0, tiled=True)  13.3 us
    ppermute x2, starting transfers between devices, to_partner(): lax.ppermute(block, 'pair', [(i, count - 1 - i) for i in range(count)])  2.03 us
    ppermute x2, waiting for transfers between devices, to_partner(): lax.ppermute(block, 'pair', [(i, count - 1 - i) for i in range(count)])  1.86 us
    pallas_call x1, Pallas kernels, copies_of(): pl.pallas_call(kernel, out_shape=jax.ShapeDtypeStruct((count, rows, 2 * H...  1.6 us
  transfers between devices with their start and end apart: 5, of which 4 were waited for; matrix products, arithmetic and copies ran while one was open for 2% of the time, Pallas kernels for 12%

profile of v6, /device:TPU:160, one launch (start us, length us, event | category | flops | bytes accessed | tf_op | source)
XLA Modules:
  0.0 72.0 jit_solution(16908917382064987005)
XLA Ops:
  0.6 1.6 %copies.1 = bf16[16,64,256]{2,1,0:T(8,128)(2,1)} custom-call(bf16[64,128]{1,0:T(8,128)(2,1)} %k.1, bf16[64,128]{1,0:T(8,128)(2,1)} %v.1), custom_call_target="tpu_custom_call" | custom-call | flops 1000000 | tf_op jit(solution)/shard_map/copies/pallas_call | solution.py:293
  2.2 0.0 copy-start.6
  2.2 0.0 copy-start
  2.2 0.0 copy-start.1
  2.2 0.0 copy-start.2
  2.3 0.0 copy-start.3
  2.3 7.2 %all-to-all-start = ((bf16[16,64,256]{2,1,0:T(8,128)(2,1)}), bf16[16,64,256]{2,1,0:T(8,128)(2,1)S(1)}, u32[]{:S(2)}, u32[]{:S(2)}) async-start(bf16[16,64,256]{2,1,0:T(8,128)(2,1)} %copies.1), calls=%async_computation | async-start | bytes 1048576 | tf_op jit(solution)/shard_map/all_to_all | solution.py:327
  9.5 0.0 copy-start.4
  9.5 0.0 copy-start.5
  10.1 0.0 copy-done.6
  10.1 0.6 dynamic_slice.4
  10.7 0.7 %pad_add_fusion.refs_0_.place = s32[4]{0:T(128)S(1)} fusion(s32[1]{0:T(128)} %dynamic_slice.4, s32[1]{0:T(128)S(6)} %copy.20, s32[1]{0:T(128)} %bitcast.1, s32[1]{0:T(128)} %bitcast), kind=kLoop, calls=%fused_computation.1 | loop fusion | flops 12 | bytes 32 | tf_op jit(solution)/shard_map/stack | solution.py:353
  11.5 0.0 copy-done
  11.5 0.0 copy-done.1
  11.5 0.0 copy-done.2
  11.5 0.0 copy-done.3
  11.5 0.0 copy-done.4
  11.5 0.0 copy-done.5
  11.5 1.5 %prepare.1 = (bf16[128,1024]{1,0:T(8,128)(2,1)S(1)}, bf16[1024,256]{1,0:T(8,128)(2,1)S(1)}, bf16[16,64,256]{2,1,0:T(8,128)(2,1)}) custom-call(s32[4]{0:T(128)S(1)} %pad_add_fusion.refs_0_.place, bf16[64,1024]{1,0:T(8,128)(2,1)S(1)} %copy-done, bf16[64,1024]{1,0:T(8,128)(2,1)S(1)} %bitcast.10, bf16[64,1024]{1,0:T(8,128)(2,1)S(1)} %copy-done.2, ...), custom_call_target="tpu_custom_call" | custom-call | flops 1000000000 | tf_op jit(solution)/shard_map/prepare/pallas_call | solution.py:272
  13.0 8.0 %all-to-all-done.kv = bf16[16,64,256]{2,1,0:T(8,128)(2,1)S(1)} async-done(((bf16[16,64,256]{2,1,0:T(8,128)(2,1)}), bf16[16,64,256]{2,1,0:T(8,128)(2,1)S(1)}, u32[]{:S(2)}, u32[]{:S(2)}) %all-to-all-start) | async-done | bytes 524320 | tf_op jit(solution)/shard_map/all_to_all | solution.py:327
  20.9 1.0 %collective-permute-start = (bf16[16,64,256]{2,1,0:T(8,128)(2,1)S(1)}, bf16[16,64,256]{2,1,0:T(8,128)(2,1)S(1)}, u32[]{:S(2)}, u32[]{:S(2)}) collective-permute-start(bf16[16,64,256]{2,1,0:T(8,128)(2,1)S(1)} %all-to-all-done.kv), channel_id=1, source_target_pairs={{0,128},{128,0},{1,129},{129,1},{2,130},{130,2},{3,131},{131,3},{4... | collective-permute-start | bytes 1572872 | tf_op jit(solution)/shard_map/ppermute | solution.py:332
  21.9 3.6 %all-to-all-start.1 = ((bf16[16,64,256]{2,1,0:T(8,128)(2,1)}), bf16[16,64,256]{2,1,0:T(8,128)(2,1)S(1)}, u32[]{:S(2)}, u32[]{:S(2)}) async-start(bf16[16,64,256]{2,1,0:T(8,128)(2,1)} %get-tuple-element.36), calls=%async_computation.1 | async-start | bytes 1048576 | tf_op jit(solution)/shard_map/all_to_all | solution.py:327
  25.5 2.6 %own_forward.1 = (f32[128,1024]{1,0:T(8,128)S(1)}, f32[8,1024]{1,0:T(8,128)S(1)}) custom-call(s32[4]{0:T(128)S(1)} %pad_add_fusion.refs_0_.place, bf16[128,1024]{1,0:T(8,128)(2,1)S(1)} %get-tuple-element.33.q_t, bf16[16,64,256]{2,1,0:T(8,128)(2,1)S(1)} %all-to-all-done.kv), custom_call_target="tpu_custom_call" | custom-call | flops 1073741824 | tf_op jit(solution)/shard_map/own_forward/pallas_call | solution.py:272
  28.1 7.5 %all-to-all-done.1.answer_kv = bf16[16,64,256]{2,1,0:T(8,128)(2,1)S(1)} async-done(((bf16[16,64,256]{2,1,0:T(8,128)(2,1)}), bf16[16,64,256]{2,1,0:T(8,128)(2,1)S(1)}, u32[]{:S(2)}, u32[]{:S(2)}) %all-to-all-start.1) | async-done | bytes 524320 | tf_op jit(solution)/shard_map/all_to_all | solution.py:327
  35.6 0.0 collective-permute-done.kv
  35.6 7.6 %other.1 = (bf16[64,1024]{1,0:T(8,128)(2,1)}, bf16[64,1024]{1,0:T(8,128)(2,1)}, bf16[16,64,256]{2,1,0:T(8,128)(2,1)S(1)}, bf16[16,64,256]{2,1,0:T(8,128)(2,1)}, ...) custom-call(s32[4]{0:T(128)S(1)} %pad_add_fusion.refs_0_.place, ...), custom_call_target="tpu_custom_call", output_to_operand_aliasing={{4}: (5, {})} | custom-call | flops 2147483648 | tf_op jit(solution)/shard_map/other/pallas_call | solution.py:272
  43.2 1.0 %collective-permute-start.1 = (bf16[16,64,256]{2,1,0:T(8,128)(2,1)S(1)}, bf16[16,64,256]{2,1,0:T(8,128)(2,1)S(1)}, u32[]{:S(2)}, u32[]{:S(2)}) collective-permute-start(bf16[16,64,256]{2,1,0:T(8,128)(2,1)S(1)} %get-tuple-element.45), channel_id=1, source_target_pairs={{0,128},{128,0},{1,129},{129,1},{2,130},{130,2},{3,131},{131,3},{4... | collective-permute-start | bytes 1572872 | tf_op jit(solution)/shard_map/ppermute | solution.py:332
  44.2 3.6 %all-to-all-start.3 = ((bf16[16,64,256]{2,1,0:T(8,128)(2,1)}), bf16[16,64,256]{2,1,0:T(8,128)(2,1)S(1)}, u32[]{:S(2)}, u32[]{:S(2)}) async-start(bf16[16,64,256]{2,1,0:T(8,128)(2,1)} %get-tuple-element.46), calls=%async_computation.3 | async-start | bytes 1048576 | tf_op jit(solution)/shard_map/all_to_all | solution.py:327
  47.8 4.6 %own_backward.1 = (bf16[64,1024]{1,0:T(8,128)(2,1)}, bf16[64,1024]{1,0:T(8,128)(2,1)}, f32[16,64,256]{2,1,0:T(8,128)S(1)}) custom-call(s32[4]{0:T(128)S(1)} %pad_add_fusion.refs_0_.place, bf16[1024,256]{1,0:T(8,128)(2,1)S(1)} %get-tuple-element.34.both_s, bf16[16,64,256]{2,1,0:T(8,128)(2,1)S(1)} %all-to-all-done.kv, ...), custom_call_target="tpu_custom_call" | custom-call | flops 1610612736 | tf_op jit(solution)/shard_map/own_backward/pallas_call | solution.py:272
  52.4 1.9 %collective-permute-done.1 = bf16[16,64,256]{2,1,0:T(8,128)(2,1)S(1)} collective-permute-done((bf16[16,64,256]{2,1,0:T(8,128)(2,1)S(1)}, bf16[16,64,256]{2,1,0:T(8,128)(2,1)S(1)}, u32[]{:S(2)}, u32[]{:S(2)}) %collective-permute-start.1) | collective-permute-done | bytes 524320 | tf_op jit(solution)/shard_map/ppermute | solution.py:332
  54.3 0.2 add_convert_fusion
  54.4 3.4 %all-to-all-done.3.answer_parts = bf16[16,64,256]{2,1,0:T(8,128)(2,1)S(1)} async-done(((bf16[16,64,256]{2,1,0:T(8,128)(2,1)}), bf16[16,64,256]{2,1,0:T(8,128)(2,1)S(1)}, u32[]{:S(2)}, u32[]{:S(2)}) %all-to-all-start.3) | async-done | bytes 524320 | tf_op jit(solution)/shard_map/all_to_all | solution.py:327
  57.9 13.3 %all_to_all.20.prompt_parts = bf16[16,64,256]{2,1,0:T(8,128)(2,1)S(1)} all-to-all(bf16[16,64,256]{2,1,0:T(8,128)(2,1)S(1)} %add_convert_fusion), channel_id=1, replica_groups=mesh['pair'=2,'ctx'=16,'head'=8] {'ctx'}, dimensions={0} | all-to-all | bytes 1048576 | tf_op jit(solution)/shard_map/all_to_all | solution.py:327
  71.2 0.8 %collected.1 = (bf16[64,128]{1,0:T(8,128)(2,1)}, bf16[64,128]{1,0:T(8,128)(2,1)}, bf16[64,128]{1,0:T(8,128)(2,1)}, bf16[64,128]{1,0:T(8,128)(2,1)}) custom-call(bf16[16,64,256]{2,1,0:T(8,128)(2,1)S(1)} %all_to_all.20.prompt_parts, bf16[16,64,256]{2,1,0:T(8,128)(2,1)S(1)} %all-to-all-done.3.answer_parts), custom_call_target="tpu_custom_call" | custom-call | tf_op jit(solution)/shard_map/collected/pallas_call | solution.py:316
Async XLA Ops:
  2.2 7.9 %copy-start.6 = (s32[2]{0:T(128)S(1)}, s32[2]{0:T(128)}, u32[]{:S(2)}) copy-start(s32[2]{0:T(128)} %param.19) | copy-start | bytes 28
  2.2 9.2 %copy-start = (bf16[64,1024]{1,0:T(8,128)(2,1)S(1)}, bf16[64,1024]{1,0:T(8,128)(2,1)}, u32[]{:S(2)}) copy-start(bf16[64,1024]{1,0:T(8,128)(2,1)} %refs_1_.1) | copy-start | bytes 393220
  2.2 9.2 %copy-start.1 = (bf16[1,64,1024]{2,1,0:T(8,128)(2,1)S(1)}, bf16[1,64,1024]{2,1,0:T(8,128)(2,1)}, u32[]{:S(2)}) copy-start(bf16[1,64,1024]{2,1,0:T(8,128)(2,1)} %param.13) | copy-start | bytes 393220
  2.2 9.2 %copy-start.2 = (bf16[64,1024]{1,0:T(8,128)(2,1)S(1)}, bf16[64,1024]{1,0:T(8,128)(2,1)}, u32[]{:S(2)}) copy-start(bf16[64,1024]{1,0:T(8,128)(2,1)} %refs_3_.1) | copy-start | bytes 393220
  2.3 9.2 %copy-start.3 = (bf16[1,64,1024]{2,1,0:T(8,128)(2,1)S(1)}, bf16[1,64,1024]{2,1,0:T(8,128)(2,1)}, u32[]{:S(2)}) copy-start(bf16[1,64,1024]{2,1,0:T(8,128)(2,1)} %param.17) | copy-start | bytes 393220
  2.3 18.7 %all-to-all-start = ((bf16[16,64,256]{2,1,0:T(8,128)(2,1)}), bf16[16,64,256]{2,1,0:T(8,128)(2,1)S(1)}, u32[]{:S(2)}, u32[]{:S(2)}) async-start(bf16[16,64,256]{2,1,0:T(8,128)(2,1)} %copies.1), calls=%async_computation | async-start | bytes 1048576 | tf_op jit(solution)/shard_map/all_to_all | solution.py:327
  9.5 2.0 %copy-start.4 = (bf16[1,64,128]{2,1,0:T(8,128)(2,1)S(1)}, bf16[1,64,128]{2,1,0:T(8,128)(2,1)}, u32[]{:S(2)}) copy-start(bf16[1,64,128]{2,1,0:T(8,128)(2,1)} %param.14) | copy-start | bytes 49156
  9.5 2.0 %copy-start.5 = (bf16[1,64,128]{2,1,0:T(8,128)(2,1)S(1)}, bf16[1,64,128]{2,1,0:T(8,128)(2,1)}, u32[]{:S(2)}) copy-start(bf16[1,64,128]{2,1,0:T(8,128)(2,1)} %param.15) | copy-start | bytes 49156
  20.9 14.6 %collective-permute-start = (bf16[16,64,256]{2,1,0:T(8,128)(2,1)S(1)}, bf16[16,64,256]{2,1,0:T(8,128)(2,1)S(1)}, u32[]{:S(2)}, u32[]{:S(2)}) collective-permute-start(bf16[16,64,256]{2,1,0:T(8,128)(2,1)S(1)} %all-to-all-done.kv), channel_id=1, source_target_pairs={{0,128},{128,0},{1,129},{129,1},{2,130},{130,2},{3,131},{131,3},{4... | collective-permute-start | bytes 1572872 | tf_op jit(solution)/shard_map/ppermute | solution.py:332
  21.9 13.6 %all-to-all-start.1 = ((bf16[16,64,256]{2,1,0:T(8,128)(2,1)}), bf16[16,64,256]{2,1,0:T(8,128)(2,1)S(1)}, u32[]{:S(2)}, u32[]{:S(2)}) async-start(bf16[16,64,256]{2,1,0:T(8,128)(2,1)} %get-tuple-element.36), calls=%async_computation.1 | async-start | bytes 1048576 | tf_op jit(solution)/shard_map/all_to_all | solution.py:327
  43.2 11.1 %collective-permute-start.1 = (bf16[16,64,256]{2,1,0:T(8,128)(2,1)S(1)}, bf16[16,64,256]{2,1,0:T(8,128)(2,1)S(1)}, u32[]{:S(2)}, u32[]{:S(2)}) collective-permute-start(bf16[16,64,256]{2,1,0:T(8,128)(2,1)S(1)} %get-tuple-element.45), channel_id=1, source_target_pairs={{0,128},{128,0},{1,129},{129,1},{2,130},{130,2},{3,131},{131,3},{4... | collective-permute-start | bytes 1572872 | tf_op jit(solution)/shard_map/ppermute | solution.py:332
  44.2 13.6 %all-to-all-start.3 = ((bf16[16,64,256]{2,1,0:T(8,128)(2,1)}), bf16[16,64,256]{2,1,0:T(8,128)(2,1)S(1)}, u32[]{:S(2)}, u32[]{:S(2)}) async-start(bf16[16,64,256]{2,1,0:T(8,128)(2,1)} %get-tuple-element.46), calls=%async_computation.3 | async-start | bytes 1048576 | tf_op jit(solution)/shard_map/all_to_all | solution.py:327
